TPU v7x, 32 devices: a whole 2x2x4 slice. The times are simulated.
32 devices in a mesh: dp: 8 (over y, x, core), tensor: 4 (over z).
Axes of the slice: x: 2, y: 2, z: 4, core: 2. Of those that a mesh axis runs over, the one named last changes fastest.
Arguments:
- tokens: bfloat16 [16384, 768], P(('dp', 'tensor')), may hold values from -6 to 6
- starts: int32 [8, 8], P('dp'), may hold values from 0 to 2047, as said below
- w_qkv: bfloat16 [768, 2304], P(None, 'tensor'), may hold values from -0.21875 to 0.21875
- b_qkv: bfloat16 [2304], P('tensor'), may hold values from -3 to 3
- w_out: bfloat16 [768, 768], P('tensor'), may hold values from -2 to 2
- b_out: bfloat16 [768], replicated, may hold values from -3 to 3
- gain_one: bfloat16 [768], replicated, may hold values from 0.099609375 to 1.8984375
- shift_one: bfloat16 [768], replicated, may hold values from -3 to 3
- w_in: bfloat16 [768, 3072], P(None, 'tensor'), may hold values from -0.21875 to 0.21875
- b_in: bfloat16 [3072], P('tensor'), may hold values from -3 to 3
- w_two: bfloat16 [3072, 768], P('tensor'), may hold values from -0.21875 to 0.21875
- b_two: bfloat16 [768], replicated, may hold values from -3 to 3
- gain_two: bfloat16 [768], replicated, may hold values from 0.099609375 to 1.8984375
- shift_two: bfloat16 [768], replicated, may hold values from -3 to 3
- cotangent: bfloat16 [16384, 768], P(('dp', 'tensor')), may hold values from -6 to 6
Outputs:
- block_out: bfloat16 [16384, 768], P(('dp', 'tensor'))
- d_tokens: bfloat16 [16384, 768], P(('dp', 'tensor'))
- d_w_qkv: float32 [768, 2304], P(None, 'tensor')
- d_b_qkv: float32 [2304], P('tensor')
- d_w_out: float32 [768, 768], P('tensor')
- d_b_out: float32 [768], replicated
- d_gain_one: float32 [768], replicated
- d_shift_one: float32 [768], replicated
- d_w_in: float32 [768, 3072], P(None, 'tensor')
- d_b_in: float32 [3072], P('tensor')
- d_w_two: float32 [3072, 768], P('tensor')
- d_b_two: float32 [768], replicated
- d_gain_two: float32 [768], replicated
- d_shift_two: float32 [768], replicated
Inputs may be any that keep to these rules, and one draw needn't show every extreme that they name: Each row holds exactly 8 documents: its first start is 0 and its starts rise strictly. In the first row the last document is a single token.
All inputs are finite; a program needn't handle non-finite values.
Results may differ from a plain program's by a relative error of at most 0.014.
Values may be sent and summed in bfloat16 or wider, within the bound.
No kernel may reach another device: no remote copies, remote signals or barrier semaphores. Data moves between devices by JAX's collectives and lax.ppermute only.
A program may use at most 192 MiB of HBM per device.

v0:
```python
import functools
import math
import jax
import jax.numpy as jnp
from jax import lax
from jax.sharding import PartitionSpec as P

HEAD = 64
ROW_LEN = 2048
DOCS = 8
F32 = jnp.float32
BF16 = jnp.bfloat16


def dot(left, right, dims):
    return lax.dot_general(left, right, (dims, ((), ())), preferred_element_type=F32)


class Places:

    def __init__(self, dp, tensor):
        self.dp, self.tensor = (dp, tensor)
        self.row = lax.axis_index("dp")
        self.z = lax.axis_index("tensor")

    def bit(self, which):
        return self.row >> which & 1

    def swap(self, value, which):
        return lax.ppermute(value, "dp", [(d, d ^ 1 << which) for d in range(self.dp)])

    def turn(self, value, step):
        size = self.tensor
        return lax.ppermute(value, "tensor", [(k, (k + step) % size) for k in range(size)])

    def onward(self, value, step):
        size = self.tensor
        pairs = [(k, k + step) for k in range(size) if 0 <= k + step < size]
        return lax.ppermute(value, "tensor", pairs)


def pair(own, other, bit):
    return jnp.where(bit == 0, jnp.stack([own, other]), jnp.stack([other, own]))


def gather_pieces(places, piece):
    parts = [piece] + [places.turn(piece, step) for step in range(1, places.tensor)]
    half = places.tensor // 2
    first, second = (jnp.stack(parts[:half]), jnp.stack(parts[half:]))
    first = pair(first, places.swap(first, 1), places.bit(1))
    second = pair(second, places.swap(second, 2), places.bit(2))
    first = pair(first, places.swap(first, 2), places.bit(2))
    second = pair(second, places.swap(second, 1), places.bit(1))
    first = pair(first, places.swap(first, 0), places.bit(0))
    second = pair(second, places.swap(second, 0), places.bit(0))
    second = jnp.swapaxes(second, 1, 2)
    return jnp.concatenate([first, second], axis=3)


def own_rows(places, weight):
    rows = weight.shape[0] // 8
    return lax.dynamic_slice_in_dim(weight, (places.row & 7) * rows, rows, 0)


def by_shard(pieces):
    ordered = jnp.transpose(pieces, (3, 1, 2, 0, 4, 5))
    return ordered.reshape(ordered.shape[0], -1, ordered.shape[-1])


def keep_and_send(value, bit, dim):
    kept = lax.dynamic_index_in_dim(value, bit, dim, keepdims=False)
    sent = lax.dynamic_index_in_dim(value, 1 - bit, dim, keepdims=False)
    return (kept.astype(F32), sent.astype(BF16))


def reduce_pieces(places, grads, order):
    shards, rows, cols = grads.shape
    value = grads.reshape(shards, 2, 2, 2, rows // 8, cols)
    for which in (0,) + order:
        kept, sent = keep_and_send(value, places.bit(which), 1)
        value = kept + places.swap(sent, which).astype(F32)
    total = value[0]
    for step in range(1, shards):
        total = total + places.turn(value[step].astype(BF16), -step).astype(F32)
    for which in range(3, places.dp.bit_length() - 1):
        total = total + places.swap(total, which)
    low = total.astype(BF16)
    for which in order[::-1] + (0,):
        low = pair(low, places.swap(low, which), places.bit(which))
    return low.reshape(rows, cols).astype(F32)


def doc_tables(starts_row, places, count):
    spots = places.z * count + jnp.arange(count, dtype=jnp.int32)
    started = (spots[:, None] >= starts_row[None, :]).astype(jnp.int32)
    doc_ids = jnp.sum(started, axis=1) - 1
    onehot = (doc_ids[:, None] == jnp.arange(DOCS, dtype=jnp.int32)[None, :]).astype(jnp.int32)
    finish = jnp.concatenate([starts_row[1:], jnp.full((1,), ROW_LEN, jnp.int32)])
    own_start = jnp.sum(onehot * starts_row[None, :], axis=1)
    own_len = jnp.sum(onehot * (finish - starts_row)[None, :], axis=1)
    angles = 0.5 * math.pi * (spots - own_start).astype(F32) / own_len.astype(F32)
    return (angles, doc_ids)


def doc_at(starts_row, spot):
    return jnp.sum((spot >= starts_row).astype(jnp.int32)) - 1


def shift_shards(state, step):
    return jnp.roll(state, step, axis=0)


def norm_parts(rows_in):
    centred = rows_in - jnp.mean(rows_in, axis=-1, keepdims=True)
    spread = jnp.mean(centred * centred, axis=-1, keepdims=True)
    scale = lax.rsqrt(spread + 1e-05)
    return (centred * scale, scale)


def norm_back(grad, normed, scale, gain):
    e = grad * gain
    d_rows = scale * (
        e
        - jnp.mean(e, axis=-1, keepdims=True)
        - normed * jnp.mean(e * normed, axis=-1, keepdims=True)
    )
    return (d_rows, jnp.sum(grad * normed, axis=0), jnp.sum(grad, axis=0))


def gelu_parts(v):
    k = math.sqrt(2 / math.pi)
    t = jnp.tanh(k * (v + 0.044715 * v * v * v))
    slope = 0.5 * (1 + t) + 0.5 * v * (1 - t * t) * k * (1 + 3 * 0.044715 * v * v)
    return (0.5 * v * (1 + t), slope)


def on_device(
    dp,
    tensor,
    tokens,
    starts,
    w_qkv,
    b_qkv,
    w_out,
    b_out,
    gain_one,
    shift_one,
    w_in,
    b_in,
    w_two,
    b_two,
    gain_two,
    shift_two,
    cotangent,
):
    places = Places(dp, tensor)
    count = tokens.shape[0]
    width = tokens.shape[1]
    heads = w_qkv.shape[1] // (3 * HEAD)
    f = lambda a: a.astype(F32)
    qkv_all = by_shard(gather_pieces(places, own_rows(places, w_qkv)))
    rest = jnp.concatenate(
        [own_rows(places, w_out), own_rows(places, w_in), own_rows(places, w_two)]
    )
    rest_all = gather_pieces(places, rest)
    n_out, n_in = (w_out.shape[0] // 8, w_in.shape[0] // 8)
    out_all = by_shard(rest_all[..., :n_out, :])
    in_all = by_shard(rest_all[..., n_out : n_out + n_in, :])
    two_all = by_shard(rest_all[..., n_out + n_in :, :])
    biases = jnp.concatenate([b_qkv, b_in]).reshape(1, -1)
    bias_all = jnp.concatenate([biases] + [places.turn(biases, s) for s in range(1, tensor)])
    bias_qkv, bias_in = (f(bias_all[:, : b_qkv.shape[0]]), f(bias_all[:, b_qkv.shape[0] :]))
    row = starts[0]
    angles, docs = doc_tables(row, places, count)
    base = places.z * count
    first_doc, last_doc = (doc_at(row, base), doc_at(row, base + count - 1))
    opening = (docs == first_doc).astype(F32)
    tail = (docs == last_doc).astype(F32)
    spot = jnp.arange(count)
    mask = jnp.where(
        (docs[:, None] == docs[None, :]) & (spot[:, None] >= spot[None, :]),
        jnp.cos(angles[:, None] - angles[None, :]),
        0.0,
    )
    cosine, sines = (jnp.cos(angles)[:, None], jnp.sin(angles)[:, None])
    mixed = (
        jnp.einsum("td,jdc->jtc", tokens, qkv_all, preferred_element_type=F32) + bias_qkv[:, None]
    )
    parts = mixed.reshape(tensor, count, heads, 3, HEAD)
    query, key, value = (jnp.transpose(parts[:, :, :, i], (0, 2, 1, 3)) for i in range(3))
    query, key, value = (
        jax.nn.relu(query).astype(BF16),
        jax.nn.relu(key).astype(BF16),
        value.astype(BF16),
    )
    ones = jnp.ones(value.shape[:-1] + (1,), BF16)
    value_one = jnp.concatenate([value, ones], axis=-1)

    def feats(a, weight):
        return jnp.concatenate([f(a) * (cosine * weight), f(a) * (sines * weight)], axis=-1).astype(
            BF16
        )

    fq_open = feats(query, opening[:, None])
    fk_tail = feats(key, tail[:, None])
    state = jnp.einsum("jhtf,jhtv->jhfv", fk_tail, value_one, preferred_element_type=F32).astype(
        BF16
    )
    carried = jnp.zeros(state.shape, F32)
    for step in range(1, tensor):
        link = (doc_at(row, base - (step - 1) * count - 1) == first_doc).astype(F32)
        carried = carried + link * f(shift_shards(places.onward(state, step), step))
    carried = carried.astype(BF16)
    scores = jnp.einsum("jhtf,jhsf->jhts", query, key, preferred_element_type=F32) * mask
    scores = scores.astype(BF16)
    sums = jnp.einsum(
        "jhts,jhsv->jhtv", scores, value_one, preferred_element_type=F32
    ) + jnp.einsum("jhtf,jhfv->jhtv", fq_open, carried, preferred_element_type=F32)
    den_raw = sums[..., HEAD:]
    den = jnp.maximum(den_raw, 1.0)
    o = sums[..., :HEAD] / den
    attended = jnp.transpose(o, (2, 0, 1, 3)).reshape(count, width).astype(BF16)
    w_out_full = out_all.reshape(width, width)
    r1 = f(tokens) + dot(attended, w_out_full, ((1,), (0,))) + f(b_out)
    n1, s1 = norm_parts(r1)
    first = (n1 * f(gain_one) + f(shift_one)).astype(BF16)
    hidden = jnp.einsum("td,jdc->jtc", first, in_all, preferred_element_type=F32) + bias_in[:, None]
    act, slope = gelu_parts(hidden)
    act = act.astype(BF16)
    second = jnp.einsum("jtc,jcd->td", act, two_all, preferred_element_type=F32) + f(b_two)
    n2, s2 = norm_parts(f(first) + second)
    block_out = (n2 * f(gain_two) + f(shift_two)).astype(BF16)
    d_r2, d_gain_two, d_shift_two = norm_back(f(cotangent), n2, s2, f(gain_two))
    d_second = d_r2.astype(BF16)
    d_b_two = jnp.sum(f(d_second), axis=0)
    g_two = jnp.einsum("td,jtc->jdc", d_second, act, preferred_element_type=F32)
    d_w_two = reduce_pieces(places, g_two, (1, 2)).T
    d_hidden = (
        jnp.einsum("td,jcd->jtc", d_second, two_all, preferred_element_type=F32) * slope
    ).astype(BF16)
    d_b_in = jnp.sum(f(d_hidden), axis=1)
    g_in = jnp.einsum("td,jtc->jdc", first, d_hidden, preferred_element_type=F32)
    d_w_in = reduce_pieces(places, g_in, (2, 1))
    d_first = jnp.einsum("jtc,jdc->td", d_hidden, in_all, preferred_element_type=F32) + d_r2
    d_r1, d_gain_one, d_shift_one = norm_back(d_first, n1, s1, f(gain_one))
    d_branch = d_r1.astype(BF16)
    d_b_out = jnp.sum(f(d_branch), axis=0)
    g_out = dot(attended, d_branch, ((0,), (0,))).reshape(tensor, -1, width)
    d_w_out = reduce_pieces(places, g_out, (1, 2))
    g = dot(d_branch, w_out_full, ((1,), (1,))).reshape(count, tensor, heads, HEAD)
    g = jnp.transpose(g, (1, 2, 0, 3))
    d_num = g / den
    d_den = jnp.where(den_raw > 1.0, -jnp.sum(g * o, axis=-1, keepdims=True) / den, 0.0)
    d_sums = jnp.concatenate([d_num, d_den], axis=-1).astype(BF16)
    d_carried = jnp.einsum("jhtf,jhtv->jhfv", fq_open, d_sums, preferred_element_type=F32).astype(
        BF16
    )
    d_state = jnp.zeros(state.shape, F32)
    for step in range(1, tensor):
        link = (doc_at(row, base + step * count) == last_doc).astype(F32)
        d_state = d_state + link * f(shift_shards(places.onward(d_carried, -step), -step))
    d_state = d_state.astype(BF16)
    d_scores = (
        jnp.einsum("jhtv,jhsv->jhts", d_sums, value_one, preferred_element_type=F32) * mask
    ).astype(BF16)
    d_fq = (
        jnp.einsum("jhtv,jhfv->jhtf", d_sums, carried, preferred_element_type=F32)
        * opening[:, None]
    )
    d_query = jnp.einsum("jhts,jhsf->jhtf", d_scores, key, preferred_element_type=F32) + (
        d_fq[..., :HEAD] * cosine + d_fq[..., HEAD:] * sines
    )
    d_fk = (
        jnp.einsum("jhtv,jhfv->jhtf", value_one, d_state, preferred_element_type=F32)
        * tail[:, None]
    )
    d_key = jnp.einsum("jhts,jhtf->jhsf", d_scores, query, preferred_element_type=F32) + (
        d_fk[..., :HEAD] * cosine + d_fk[..., HEAD:] * sines
    )
    d_value = jnp.einsum(
        "jhts,jhtv->jhsv", scores, d_sums[..., :HEAD], preferred_element_type=F32
    ) + jnp.einsum("jhtf,jhfv->jhtv", fk_tail, d_state[..., :HEAD], preferred_element_type=F32)
    d_query = jnp.where(query > 0, d_query, 0.0)
    d_key = jnp.where(key > 0, d_key, 0.0)
    d_mixed = jnp.stack([d_query, d_key, d_value], axis=3).astype(BF16)
    d_mixed = jnp.transpose(d_mixed, (0, 2, 1, 3, 4)).reshape(tensor, count, -1)
    d_b_qkv = jnp.sum(f(d_mixed), axis=1)
    g_qkv = jnp.einsum("td,jtc->jdc", tokens, d_mixed, preferred_element_type=F32)
    d_w_qkv = reduce_pieces(places, g_qkv, (2, 1))
    d_tokens = (
        jnp.einsum("jtc,jdc->td", d_mixed, qkv_all, preferred_element_type=F32) + d_r1
    ).astype(BF16)
    shared = jnp.concatenate([d_b_out, d_gain_one, d_shift_one, d_b_two, d_gain_two, d_shift_two])
    split = jnp.concatenate([d_b_qkv, d_b_in], axis=1)
    turned = jnp.concatenate([split[::-1], split[::-1]])
    split = lax.dynamic_slice_in_dim(turned, tensor - 1 - places.z, tensor, 0)
    summed = lax.psum(jnp.concatenate([shared, split.reshape(-1)]), ("dp", "tensor"))
    d_b_out, d_gain_one, d_shift_one, d_b_two, d_gain_two, d_shift_two = jnp.split(
        summed[: 6 * width], 6
    )
    split = lax.dynamic_index_in_dim(
        summed[6 * width :].reshape(tensor, -1), places.z, 0, keepdims=False
    )
    d_b_qkv, d_b_in = (split[: b_qkv.shape[0]], split[b_qkv.shape[0] :])
    return (
        block_out,
        d_tokens,
        d_w_qkv,
        d_b_qkv,
        d_w_out,
        d_b_out,
        d_gain_one,
        d_shift_one,
        d_w_in,
        d_b_in,
        d_w_two,
        d_b_two,
        d_gain_two,
        d_shift_two,
    )


def solution(mesh):
    sizes = dict(mesh.shape)
    rows = P(("dp", "tensor"), None)
    wide, tall, cut, whole = (P(None, "tensor"), P("tensor", None), P("tensor"), P())
    in_specs = (
        rows,
        P("dp", None),
        wide,
        cut,
        tall,
        whole,
        whole,
        whole,
        wide,
        cut,
        tall,
        whole,
        whole,
        whole,
        rows,
    )
    out_specs = (
        rows,
        rows,
        wide,
        cut,
        tall,
        whole,
        whole,
        whole,
        wide,
        cut,
        tall,
        whole,
        whole,
        whole,
    )
    return jax.shard_map(
        functools.partial(on_device, sizes["dp"], sizes["tensor"]),
        mesh=mesh,
        in_specs=in_specs,
        out_specs=out_specs,
        check_vma=False,
    )
```

profile of v0, /device:TPU:1, one launch (start us, length us, event | category | flops | bytes accessed | tf_op | source)
XLA Modules:
  0.0 416.2 jit_solution(15520140502404136864)
XLA Ops:
  2.6 4.2 %collective-permute-start.20 = (bf16[216,768]{1,0:T(8,128)(2,1)S(1)}, bf16[216,768]{1,0:T(8,128)(2,1)S(1)}, u32[]{:S(2)}, u32[]{:S(2)}) collective-permute-start(bf16[216,768]{1,0:T(8,128)(2,1)S(1)} %get-tuple-element.142), channel_id=1, source_target_pairs={{0,3},{1,0},{2,1},{3,2},{4,7},{5,4},{6,5},{7,6},{8,11},{9,8},{10,9... | collective-permute-start | bytes 995336 | tf_op jit(solution)/shard_map/ppermute | solution.py:34
  7.8 2.3 collective-permute-start.10
  14.5 2.3 cosine_select_fusion
  24.0 3.8 collective-permute-start.15
  27.9 3.6 collective-permute-start.5
  31.6 4.8 %collective-permute-done.5 = bf16[96,576]{1,0:T(8,128)(2,1)S(1)} collective-permute-done((bf16[96,576]{1,0:T(8,128)(2,1)S(1)}, bf16[96,576]{1,0:T(8,128)(2,1)S(1)}, u32[]{:S(2)}, u32[]{:S(2)}) %collective-permute-start.5) | collective-permute-done | bytes 110624 | tf_op jit(solution)/shard_map/ppermute | solution.py:34
  36.5 3.1 collective-permute-start
  39.6 4.8 %collective-permute-done.4 = bf16[96,576]{1,0:T(8,128)(2,1)S(1)} collective-permute-done((bf16[96,576]{1,0:T(8,128)(2,1)S(1)}, bf16[96,576]{1,0:T(8,128)(2,1)S(1)}, u32[]{:S(2)}, u32[]{:S(2)}) %collective-permute-start.4) | collective-permute-done | bytes 110624 | tf_op jit(solution)/shard_map/ppermute | solution.py:34
  48.1 2.6 collective-permute-done.6
  54.0 20.4 %collective-permute-done.7 = bf16[2,2,96,576]{3,2,1,0:T(8,128)(2,1)S(1)} collective-permute-done((bf16[2,2,96,576]{3,2,1,0:T(8,128)(2,1)S(1)}, bf16[2,2,96,576]{3,2,1,0:T(8,128)(2,1)S(1)}, u32[]{:S(2)}, u32[]{:S(2)}) %collective-permute-start.7) | collective-permute-done | bytes 442400 | tf_op jit(solution)/shard_map/ppermute | solution.py:30
  74.7 4.7 %collective-permute-start.8 = (bf16[2,2,2,96,576]{4,3,2,1,0:T(8,128)(2,1)S(1)}, bf16[2,2,2,96,576]{4,3,2,1,0:T(8,128)(2,1)S(1)}, u32[]{:S(2)}, u32[]{:S(2)}) collective-permute-start(bf16[2,2,2,96,576]{4,3,2,1,0:T(8,128)(2,1)S(1)} %maximum_select_fusion.14), channel_id=1, source_target_pairs={{0,4},{4,0},{8,12},{12,8},{16,20},{20,16},{24,28},{28,24},{1,5},{5... | collective-permute-start | bytes 2654216 | tf_op jit(solution)/shard_map/ppermute | solution.py:30
  86.0 2.5 broadcast_add_fusion
  90.2 2.4 collective-permute-start.12
  92.6 3.7 collective-permute-start.13
  101.8 9.1 %collective-permute-done.22 = bf16[2,2,216,768]{3,2,0,1:T(8,128)(2,1)S(1)} collective-permute-done((bf16[2,2,216,768]{3,2,0,1:T(8,128)(2,1)S(1)}, bf16[2,2,216,768]{3,2,0,1:T(8,128)(2,1)S(1)}, u32[]{:S(2)}, u32[]{:S(2)}) %collective-permute-start.22) | collective-permute-done | bytes 1327136 | tf_op jit(solution)/shard_map/ppermute | solution.py:30
  110.9 2.1 maximum_select_fusion.4
  119.3 3.5 fusion.7
  122.9 3.0 pad_maximum_fusion.1
  127.4 4.8 %fusion.56 = f32[4,768,512]{1,2,0:T(8,128)} fusion(bf16[4,768,768]{2,1,0:T(8,128)(2,1)S(1)} %bitcast.427, f32[512,768]{1,0:T(8,128)S(1)} %get-tuple-element.171, f32[768]{0:T(1024)S(1)} %convert_element_type.549, f32[768]{0:T(1024)S(1)} %convert_element_type.548, f32[512]{0:T(512)S(1)} %add_rsqrt_fusion.1, f32[512]{0:T(512)S(1)} %broadcast_multiply_fusion.5), kind=kOutput, calls=%fused_computation.163 | convolution fusion | flops 2417885184 | bytes 12593152 | tf_op jit(solution)/shard_map/td,jdc->jtc/dot_general | solution.py:227
  132.2 6.3 %fusion.145 = (f32[512]{0:T(512)S(1)}, f32[512,768]{1,0:T(8,128)S(1)}) fusion(f32[768]{0:T(1024)S(1)} %convert_element_type.554, bf16[4,768,768]{2,1,0:T(8,128)(2,1)S(1)} %bitcast.431, f32[4,768,512]{1,2,0:T(8,128)} %fusion.56, f32[4,768]{1,0:T(4,128)S(1)} %fusion.96, f32[768]{0:T(1024)S(1)} %convert_element_type.549, f32[768]{0:T(1024)S(1)} %convert_element_type.548, ...), kind=kOutput, calls=%fused_computation.357 | convolution fusion | flops 2435186176 | bytes 14183424 | tf_op jit(solution)/shard_map/jtc,jcd->td/dot_general | solution.py:230
  142.0 9.2 %convert_reduce_fusion = (f32[4,768]{1,0:T(4,128)S(1)}, bf16[4,512,768]{2,1,0:T(8,128)(2,1)}) fusion(f32[4,768,512]{1,2,0:T(8,128)} %fusion.56, f32[4,768]{1,0:T(4,128)S(1)} %fusion.96, bf16[4,768,768]{2,1,0:T(8,128)(2,1)S(1)} %bitcast.432, f32[512,768]{1,0:T(8,128)S(1)} %get-tuple-element.97), kind=kOutput, calls=%fused_computation.12 | convolution fusion | flops 2450912256 | bytes 15753216 | tf_op jit(solution)/shard_map/td,jcd->jtc/dot_general | solution.py:239
  151.1 5.0 %multiply_reduce_fusion = (f32[768]{0:T(1024)S(1)}, f32[512]{0:T(512)S(1)}, f32[512]{0:T(512)S(1)}, f32[768]{0:T(1024)S(1)}, f32[512,768]{1,0:T(8,128)S(1)}) fusion(f32[512,768]{1,0:T(8,128)S(1)} %get-tuple-element.171, f32[512]{0:T(512)S(1)} %add_rsqrt_fusion.1, f32[512]{0:T(512)S(1)} %broadcast_multiply_fusion.5, f32[768]{0:T(1024)S(1)} %convert_element_type.548, ...), kind=kOutput, calls=%fused_computation.99 | convolution fusion | flops 2419848704 | bytes 12600320 | tf_op jit(solution)/shard_map/jtc,jdc->td/dot_general | solution.py:244
  166.4 5.3 %fusion.54 = f32[4,768,768]{1,2,0:T(8,128)} fusion(bf16[4,512,768]{2,1,0:T(8,128)(2,1)S(1)} %copy-done.23, f32[512,768]{1,0:T(8,128)S(1)} %get-tuple-element.171, f32[768]{0:T(1024)S(1)} %convert_element_type.549, f32[768]{0:T(1024)S(1)} %convert_element_type.548, f32[512]{0:T(512)S(1)} %add_rsqrt_fusion.1, f32[512]{0:T(512)S(1)} %broadcast_multiply_fusion.5), kind=kOutput, calls=%fused_computation.161 | convolution fusion | flops 2417885184 | bytes 14166016 | tf_op jit(solution)/shard_map/td,jtc->jdc/dot_general | solution.py:242
  171.7 5.2 %fusion.51 = f32[4,768,768]{1,2,0:T(8,128)S(1)} fusion(f32[512,768]{1,0:T(8,128)S(1)} %get-tuple-element.97, f32[4,768,512]{1,2,0:T(8,128)} %fusion.56, f32[4,768]{1,0:T(4,128)S(1)} %fusion.96), kind=kOutput, calls=%fused_computation.158 | convolution fusion | flops 2432040960 | bytes 17313792 | tf_op jit(solution)/shard_map/td,jtc->jdc/dot_general | solution.py:236
  176.9 2.7 convolution_multiply_fusion.1
  183.6 4.2 %fusion.8 = bf16[4,2,2,96,768]{4,3,0,2,1:T(8,128)(2,1)} fusion(f32[4,2,2,2,96,768]{5,4,3,2,1,0:T(8,128)} %bitcast.421, s32[]{:T(128)S(6)} %select_n.542), kind=kLoop, calls=%fused_computation.37 | loop fusion | bytes 4718596 | tf_op jit(solution)/shard_map/convert_element_type | solution.py:73
  200.5 4.9 %convolution_bitcast_fusion = f32[4,768,576]{1,2,0:T(8,128)} fusion(bf16[4,512,576]{1,2,0:T(8,128)(2,1)S(1)} %bitcast.412, bf16[512,768]{1,0:T(8,128)(2,1)S(1)} %copy-done.16), kind=kOutput, calls=%fused_computation.27 | convolution fusion | flops 1811939328 | bytes 10223616 | tf_op jit(solution)/shard_map/td,jtc->jdc/dot_general | solution.py:288
  205.3 8.5 %copy.194 = f32[4,768,576]{2,1,0:T(8,128)} copy(f32[4,768,576]{1,2,0:T(8,128)} %convolution_bitcast_fusion) | data formatting | bytes 14155776 | tf_op jit(solution)/shard_map/td,jtc->jdc/transpose | solution.py:288
  213.9 5.9 %fusion.33 = bf16[512,768]{1,0:T(8,128)(2,1)} fusion(f32[512,768]{1,0:T(8,128)} %copy-done.4, bf16[4,512,576]{1,2,0:T(8,128)(2,1)S(1)} %bitcast.413, bf16[4,768,576]{2,1,0:T(8,128)(2,1)} %bitcast.434), kind=kOutput, calls=%fused_computation.90 | convolution fusion | flops 1812725760 | bytes 8257536 | tf_op jit(solution)/shard_map/jtc,jdc->td/dot_general | solution.py:291
  222.3 3.6 fusion.13
  227.0 2.3 collective-permute-done.37
  230.0 3.4 collective-permute-done.38
  233.5 2.2 collective-permute-start.41
  235.7 4.6 %collective-permute-start.40 = (bf16[24,768]{1,0:T(8,128)(2,1)S(1)}, bf16[24,768]{1,0:T(8,128)(2,1)S(1)}, u32[]{:S(2)}, u32[]{:S(2)}) collective-permute-start(bf16[24,768]{1,0:T(8,128)(2,1)S(1)} %get-tuple-element.155), channel_id=1, source_target_pairs={{0,2},{1,3},{2,0},{3,1},{4,6},{5,7},{6,4},{7,5},{8,10},{9,11},{10,... | collective-permute-start | bytes 110600 | tf_op jit(solution)/shard_map/ppermute | solution.py:34
  240.3 41.7 %psum.7 = f32[9984]{0:T(1024)S(1)} all-reduce(f32[9984]{0:T(1024)S(1)} %constant_dynamic-update-slice_fusion), channel_id=1, replica_groups=mesh['dp'=8,'tensor'=4] {'dp','tensor'}, use_global_device_ids=true, to_apply=%region_28.29 | all-reduce | flops 9984 | bytes 79872 | tf_op jit(solution)/shard_map/psum | solution.py:297
  283.6 2.1 collective-permute-start.42
  288.9 3.1 bitcast_add_fusion.2
  296.0 3.7 bitcast_add_fusion.1
  299.7 14.8 %collective-permute-done.28 = bf16[4,2,96,576]{3,2,1,0:T(8,128)(2,1)S(1)} collective-permute-done((bf16[4,2,96,576]{3,2,1,0:T(8,128)(2,1)S(1)}, bf16[4,2,96,576]{3,2,1,0:T(8,128)(2,1)S(1)}, u32[]{:S(2)}, u32[]{:S(2)}) %collective-permute-start.28) | collective-permute-done | bytes 884768 | tf_op jit(solution)/shard_map/ppermute | solution.py:30
  316.4 9.3 %collective-permute-done.29 = bf16[4,96,576]{2,1,0:T(8,128)(2,1)S(1)} collective-permute-done((bf16[4,96,576]{2,1,0:T(8,128)(2,1)S(1)}, bf16[4,96,576]{2,1,0:T(8,128)(2,1)S(1)}, u32[]{:S(2)}, u32[]{:S(2)}) %collective-permute-start.29) | collective-permute-done | bytes 442400 | tf_op jit(solution)/shard_map/ppermute | solution.py:30
  331.6 2.3 collective-permute-done.31
  336.2 19.9 %collective-permute-done.33 = bf16[96,576]{1,0:T(8,128)(2,1)S(1)} collective-permute-done((bf16[96,576]{1,0:T(8,128)(2,1)S(1)}, bf16[96,576]{1,0:T(8,128)(2,1)S(1)}, u32[]{:S(2)}, u32[]{:S(2)}) %collective-permute-start.33) | collective-permute-done | bytes 110624 | tf_op jit(solution)/shard_map/ppermute | solution.py:30
  361.4 8.6 %collective-permute-start.35 = (bf16[2,2,96,576]{3,2,1,0:T(8,128)(2,1)S(1)}, bf16[2,2,96,576]{3,2,1,0:T(8,128)(2,1)S(1)}, u32[]{:S(2)}, u32[]{:S(2)}) collective-permute-start(bf16[2,2,96,576]{3,2,1,0:T(8,128)(2,1)S(1)} %maximum_select_fusion.24), channel_id=1, source_target_pairs={{0,4},{4,0},{8,12},{12,8},{16,20},{20,16},{24,28},{28,24},{1,5},{5... | collective-permute-start | bytes 1327112 | tf_op jit(solution)/shard_map/ppermute | solution.py:30
  372.2 2.3 collective-permute-start.48
  378.4 6.6 %collective-permute-done.49 = bf16[96,768]{1,0:T(8,128)(2,1)S(1)} collective-permute-done((bf16[96,768]{1,0:T(8,128)(2,1)S(1)}, bf16[96,768]{1,0:T(8,128)(2,1)S(1)}, u32[]{:S(2)}, u32[]{:S(2)}) %collective-permute-start.49) | collective-permute-done | bytes 147488 | tf_op jit(solution)/shard_map/ppermute | solution.py:34
  386.0 9.7 %collective-permute-done.58 = bf16[96,768]{1,0:T(8,128)(2,1)S(1)} collective-permute-done((bf16[96,768]{1,0:T(8,128)(2,1)S(1)}, bf16[96,768]{1,0:T(8,128)(2,1)S(1)}, u32[]{:S(2)}, u32[]{:S(2)}) %collective-permute-start.58) | collective-permute-done | bytes 147488 | tf_op jit(solution)/shard_map/ppermute | solution.py:34
  400.5 6.5 %collective-permute-done.52 = bf16[2,96,768]{2,1,0:T(8,128)(2,1)S(1)} collective-permute-done((bf16[2,96,768]{2,1,0:T(8,128)(2,1)S(1)}, bf16[2,96,768]{2,1,0:T(8,128)(2,1)S(1)}, u32[]{:S(2)}, u32[]{:S(2)}) %collective-permute-start.52) | collective-permute-done | bytes 294944 | tf_op jit(solution)/shard_map/ppermute | solution.py:30
  407.1 2.2 collective-permute-start.53
  (343 shorter events, 114.6 us)
Async XLA Ops:
  2.6 44.6 %collective-permute-start.20 = (bf16[216,768]{1,0:T(8,128)(2,1)S(1)}, bf16[216,768]{1,0:T(8,128)(2,1)S(1)}, u32[]{:S(2)}, u32[]{:S(2)}) collective-permute-start(bf16[216,768]{1,0:T(8,128)(2,1)S(1)} %get-tuple-element.142), channel_id=1, source_target_pairs={{0,3},{1,0},{2,1},{3,2},{4,7},{5,4},{6,5},{7,6},{8,11},{9,8},{10,9... | collective-permute-start | bytes 995336 | tf_op jit(solution)/shard_map/ppermute | solution.py:34
  6.8 40.4 %collective-permute-start.19 = (bf16[216,768]{1,0:T(8,128)(2,1)S(1)}, bf16[216,768]{1,0:T(8,128)(2,1)S(1)}, u32[]{:S(2)}, u32[]{:S(2)}) collective-permute-start(bf16[216,768]{1,0:T(8,128)(2,1)S(1)} %get-tuple-element.142), channel_id=1, source_target_pairs={{0,2},{1,3},{2,0},{3,1},{4,6},{5,7},{6,4},{7,5},{8,10},{9,11},{10,... | collective-permute-start | bytes 995336 | tf_op jit(solution)/shard_map/ppermute | solution.py:34
  7.6 16.4 %collective-permute-start.11 = (bf16[1,1344]{1,0:T(2,128)(2,1)S(1)}, bf16[1,1344]{1,0:T(2,128)(2,1)S(1)}, u32[]{:S(2)}, u32[]{:S(2)}) collective-permute-start(bf16[1,1344]{1,0:T(2,128)(2,1)S(1)} %reshape.1789), channel_id=1, source_target_pairs={{0,3},{1,0},{2,1},{3,2},{4,7},{5,4},{6,5},{7,6},{8,11},{9,8},{10,9... | collective-permute-start | bytes 8072 | tf_op jit(solution)/shard_map/ppermute | solution.py:34
  7.8 20.1 %collective-permute-start.10 = (bf16[1,1344]{1,0:T(2,128)(2,1)S(1)}, bf16[1,1344]{1,0:T(2,128)(2,1)S(1)}, u32[]{:S(2)}, u32[]{:S(2)}) collective-permute-start(bf16[1,1344]{1,0:T(2,128)(2,1)S(1)} %reshape.1789), channel_id=1, source_target_pairs={{0,2},{1,3},{2,0},{3,1},{4,6},{5,7},{6,4},{7,5},{8,10},{9,11},{10,... | collective-permute-start | bytes 8072 | tf_op jit(solution)/shard_map/ppermute | solution.py:34
  10.1 21.4 %collective-permute-start.9 = (bf16[1,1344]{1,0:T(2,128)(2,1)S(1)}, bf16[1,1344]{1,0:T(2,128)(2,1)S(1)}, u32[]{:S(2)}, u32[]{:S(2)}) collective-permute-start(bf16[1,1344]{1,0:T(2,128)(2,1)S(1)} %reshape.1789), channel_id=1, source_target_pairs={{0,1},{1,2},{2,3},{3,0},{4,5},{5,6},{6,7},{7,4},{8,9},{9,10},{10,1... | collective-permute-start | bytes 8072 | tf_op jit(solution)/shard_map/ppermute | solution.py:34
  24.0 23.6 %collective-permute-start.15 = (bf16[216,768]{1,0:T(8,128)(2,1)S(1)}, bf16[216,768]{1,0:T(8,128)(2,1)S(1)}, u32[]{:S(2)}, u32[]{:S(2)}) collective-permute-start(bf16[216,768]{1,0:T(8,128)(2,1)S(1)} %get-tuple-element.142), channel_id=1, source_target_pairs={{0,1},{1,2},{2,3},{3,0},{4,5},{5,6},{6,7},{7,4},{8,9},{9,10},{10,1... | collective-permute-start | bytes 995336 | tf_op jit(solution)/shard_map/ppermute | solution.py:34
  27.9 8.6 %collective-permute-start.5 = (bf16[96,576]{1,0:T(8,128)(2,1)S(1)}, bf16[96,576]{1,0:T(8,128)(2,1)S(1)}, u32[]{:S(2)}, u32[]{:S(2)}) collective-permute-start(bf16[96,576]{1,0:T(8,128)(2,1)S(1)} %copy.217), channel_id=1, source_target_pairs={{0,3},{1,0},{2,1},{3,2},{4,7},{5,4},{6,5},{7,6},{8,11},{9,8},{10,9... | collective-permute-start | bytes 331784 | tf_op jit(solution)/shard_map/ppermute | solution.py:34
  31.5 13.0 %collective-permute-start.4 = (bf16[96,576]{1,0:T(8,128)(2,1)S(1)}, bf16[96,576]{1,0:T(8,128)(2,1)S(1)}, u32[]{:S(2)}, u32[]{:S(2)}) collective-permute-start(bf16[96,576]{1,0:T(8,128)(2,1)S(1)} %copy.217), channel_id=1, source_target_pairs={{0,2},{1,3},{2,0},{3,1},{4,6},{5,7},{6,4},{7,5},{8,10},{9,11},{10,... | collective-permute-start | bytes 331784 | tf_op jit(solution)/shard_map/ppermute | solution.py:34
  36.5 9.3 %collective-permute-start = (bf16[96,576]{1,0:T(8,128)(2,1)S(1)}, bf16[96,576]{1,0:T(8,128)(2,1)S(1)}, u32[]{:S(2)}, u32[]{:S(2)}) collective-permute-start(bf16[96,576]{1,0:T(8,128)(2,1)S(1)} %copy.217), channel_id=1, source_target_pairs={{0,1},{1,2},{2,3},{3,0},{4,5},{5,6},{6,7},{7,4},{8,9},{9,10},{10,1... | collective-permute-start | bytes 331784 | tf_op jit(solution)/shard_map/ppermute | solution.py:34
  47.3 33.1 %collective-permute-start.21 = (bf16[2,216,768]{2,1,0:T(8,128)(2,1)S(1)}, bf16[2,216,768]{2,1,0:T(8,128)(2,1)S(1)}, u32[]{:S(2)}, u32[]{:S(2)}) collective-permute-start(bf16[2,216,768]{2,1,0:T(8,128)(2,1)S(1)} %get-tuple-element.131), channel_id=1, source_target_pairs={{0,16},{4,20},{8,24},{12,28},{16,0},{20,4},{24,8},{28,12},{1,17},{... | collective-permute-start | bytes 1990664 | tf_op jit(solution)/shard_map/ppermute | solution.py:30
  47.8 34.1 %collective-permute-start.16 = (bf16[2,216,768]{2,1,0:T(8,128)(2,1)S(1)}, bf16[2,216,768]{2,1,0:T(8,128)(2,1)S(1)}, u32[]{:S(2)}, u32[]{:S(2)}) collective-permute-start(bf16[2,216,768]{2,1,0:T(8,128)(2,1)S(1)} %get-tuple-element.128), channel_id=1, source_target_pairs={{0,8},{4,12},{8,0},{12,4},{16,24},{20,28},{24,16},{28,20},{1,9},{5... | collective-permute-start | bytes 1990664 | tf_op jit(solution)/shard_map/ppermute | solution.py:30
  50.8 23.6 %collective-permute-start.7 = (bf16[2,2,96,576]{3,2,1,0:T(8,128)(2,1)S(1)}, bf16[2,2,96,576]{3,2,1,0:T(8,128)(2,1)S(1)}, u32[]{:S(2)}, u32[]{:S(2)}) collective-permute-start(bf16[2,2,96,576]{3,2,1,0:T(8,128)(2,1)S(1)} %maximum_select_fusion.22), channel_id=1, source_target_pairs={{0,8},{4,12},{8,0},{12,4},{16,24},{20,28},{24,16},{28,20},{1,9},{5... | collective-permute-start | bytes 1327112 | tf_op jit(solution)/shard_map/ppermute | solution.py:30
  52.2 27.2 %collective-permute-start.2 = (bf16[2,2,96,576]{3,2,1,0:T(8,128)(2,1)S(1)}, bf16[2,2,96,576]{3,2,1,0:T(8,128)(2,1)S(1)}, u32[]{:S(2)}, u32[]{:S(2)}) collective-permute-start(bf16[2,2,96,576]{3,2,1,0:T(8,128)(2,1)S(1)} %maximum_select_fusion.20), channel_id=1, source_target_pairs={{0,16},{4,20},{8,24},{12,28},{16,0},{20,4},{24,8},{28,12},{1,17},{... | collective-permute-start | bytes 1327112 | tf_op jit(solution)/shard_map/ppermute | solution.py:30
  74.7 8.6 %collective-permute-start.8 = (bf16[2,2,2,96,576]{4,3,2,1,0:T(8,128)(2,1)S(1)}, bf16[2,2,2,96,576]{4,3,2,1,0:T(8,128)(2,1)S(1)}, u32[]{:S(2)}, u32[]{:S(2)}) collective-permute-start(bf16[2,2,2,96,576]{4,3,2,1,0:T(8,128)(2,1)S(1)} %maximum_select_fusion.14), channel_id=1, source_target_pairs={{0,4},{4,0},{8,12},{12,8},{16,20},{20,16},{24,28},{28,24},{1,5},{5... | collective-permute-start | bytes 2654216 | tf_op jit(solution)/shard_map/ppermute | solution.py:30
  80.6 30.3 %collective-permute-start.22 = (bf16[2,2,216,768]{3,2,0,1:T(8,128)(2,1)S(1)}, bf16[2,2,216,768]{3,2,0,1:T(8,128)(2,1)S(1)}, u32[]{:S(2)}, u32[]{:S(2)}) collective-permute-start(bf16[2,2,216,768]{3,2,0,1:T(8,128)(2,1)S(1)} %maximum_select_fusion.9), channel_id=1, source_target_pairs={{0,8},{4,12},{8,0},{12,4},{16,24},{20,28},{24,16},{28,20},{1,9},{5... | collective-permute-start | bytes 3981320 | tf_op jit(solution)/shard_map/ppermute | solution.py:30
  82.1 32.5 %collective-permute-start.17 = (bf16[2,2,216,768]{3,2,1,0:T(8,128)(2,1)S(1)}, bf16[2,2,216,768]{3,2,1,0:T(8,128)(2,1)S(1)}, u32[]{:S(2)}, u32[]{:S(2)}) collective-permute-start(bf16[2,2,216,768]{3,2,1,0:T(8,128)(2,1)S(1)} %maximum_select_fusion.8), channel_id=1, source_target_pairs={{0,16},{4,20},{8,24},{12,28},{16,0},{20,4},{24,8},{28,12},{1,17},{... | collective-permute-start | bytes 3981320 | tf_op jit(solution)/shard_map/ppermute | solution.py:30
  90.2 24.3 %collective-permute-start.12 = (bf16[4,3,128,65]{2,3,1,0:T(8,128)(2,1)S(1)}, bf16[4,3,128,65]{2,3,1,0:T(8,128)(2,1)S(1)}, u32[]{:S(2)}, u32[]{:S(2)}) collective-permute-start(bf16[4,3,128,65]{2,3,1,0:T(8,128)(2,1)S(1)} %convolution_convert_fusion.1), channel_id=1, source_target_pairs={{0,1},{1,2},{2,3},{4,5},{5,6},{6,7},{8,9},{9,10},{10,11},{12,13},{... | collective-permute-start | bytes 599048 | tf_op jit(solution)/shard_map/ppermute | solution.py:39
  92.6 23.7 %collective-permute-start.13 = (bf16[4,3,128,65]{2,3,1,0:T(8,128)(2,1)S(1)}, bf16[4,3,128,65]{2,3,1,0:T(8,128)(2,1)S(1)}, u32[]{:S(2)}, u32[]{:S(2)}) collective-permute-start(bf16[4,3,128,65]{2,3,1,0:T(8,128)(2,1)S(1)} %convolution_convert_fusion.1), channel_id=1, source_target_pairs={{0,2},{1,3},{4,6},{5,7},{8,10},{9,11},{12,14},{13,15},{16,18},{17,... | collective-permute-start | bytes 599048 | tf_op jit(solution)/shard_map/ppermute | solution.py:39
  96.3 18.2 %collective-permute-start.14 = (bf16[4,3,128,65]{2,3,1,0:T(8,128)(2,1)S(1)}, bf16[4,3,128,65]{2,3,1,0:T(8,128)(2,1)S(1)}, u32[]{:S(2)}, u32[]{:S(2)}) collective-permute-start(bf16[4,3,128,65]{2,3,1,0:T(8,128)(2,1)S(1)} %convolution_convert_fusion.1), channel_id=1, source_target_pairs={{0,3},{4,7},{8,11},{12,15},{16,19},{20,23},{24,27},{28,31}} | collective-permute-start | bytes 599048 | tf_op jit(solution)/shard_map/ppermute | solution.py:39
  116.3 6.6 %collective-permute-start.18 = (bf16[2,2,2,216,768]{4,3,2,1,0:T(8,128)(2,1)}, bf16[2,2,2,216,768]{4,3,2,1,0:T(8,128)(2,1)S(1)}, u32[]{:S(2)}, u32[]{:S(2)}) collective-permute-start(bf16[2,2,2,216,768]{4,3,2,1,0:T(8,128)(2,1)} %maximum_select_fusion.3), channel_id=1, source_target_pairs={{0,4},{4,0},{8,12},{12,8},{16,20},{20,16},{24,28},{28,24},{1,5},{5... | collective-permute-start | bytes 7962632 | tf_op jit(solution)/shard_map/ppermute | solution.py:30
  160.3 31.5 %collective-permute-start.24 = (bf16[4,3,128,65]{2,3,1,0:T(8,128)(2,1)}, bf16[4,3,128,65]{2,3,1,0:T(8,128)(2,1)}, u32[]{:S(2)}, u32[]{:S(2)}) collective-permute-start(bf16[4,3,128,65]{2,3,1,0:T(8,128)(2,1)} %convolution_convert_fusion), channel_id=1, source_target_pairs={{1,0},{2,1},{3,2},{5,4},{6,5},{7,6},{9,8},{10,9},{11,10},{13,12},{... | collective-permute-start | bytes 599048 | tf_op jit(solution)/shard_map/ppermute | solution.py:39
  161.8 33.6 %collective-permute-start.25 = (bf16[4,3,128,65]{2,3,1,0:T(8,128)(2,1)}, bf16[4,3,128,65]{2,3,1,0:T(8,128)(2,1)}, u32[]{:S(2)}, u32[]{:S(2)}) collective-permute-start(bf16[4,3,128,65]{2,3,1,0:T(8,128)(2,1)} %convolution_convert_fusion), channel_id=1, source_target_pairs={{2,0},{3,1},{6,4},{7,5},{10,8},{11,9},{14,12},{15,13},{18,16},{19,... | collective-permute-start | bytes 599048 | tf_op jit(solution)/shard_map/ppermute | solution.py:39
  163.1 30.5 %collective-permute-start.26 = (bf16[4,3,128,65]{2,3,1,0:T(8,128)(2,1)}, bf16[4,3,128,65]{2,3,1,0:T(8,128)(2,1)}, u32[]{:S(2)}, u32[]{:S(2)}) collective-permute-start(bf16[4,3,128,65]{2,3,1,0:T(8,128)(2,1)} %convolution_convert_fusion), channel_id=1, source_target_pairs={{3,0},{7,4},{11,8},{15,12},{19,16},{23,20},{27,24},{31,28}} | collective-permute-start | bytes 599048 | tf_op jit(solution)/shard_map/ppermute | solution.py:39
  183.3 36.5 %collective-permute-start.36 = (bf16[4,2,2,24,768]{4,3,2,1,0:T(8,128)(2,1)}, bf16[4,2,2,24,768]{4,3,2,1,0:T(8,128)(2,1)}, u32[]{:S(2)}, u32[]{:S(2)}) collective-permute-start(bf16[4,2,2,24,768]{4,3,2,1,0:T(8,128)(2,1)} %fusion.68), channel_id=1, source_target_pairs={{0,4},{4,0},{8,12},{12,8},{16,20},{20,16},{24,28},{28,24},{1,5},{5... | collective-permute-start | bytes 1769480 | tf_op jit(solution)/shard_map/ppermute | solution.py:30
  187.8 108.1 %collective-permute-start.45 = (bf16[4,2,2,96,768]{4,3,0,2,1:T(8,128)(2,1)}, bf16[4,2,2,96,768]{4,3,0,2,1:T(8,128)(2,1)}, u32[]{:S(2)}, u32[]{:S(2)}) collective-permute-start(bf16[4,2,2,96,768]{4,3,0,2,1:T(8,128)(2,1)} %fusion.8), channel_id=1, source_target_pairs={{0,4},{4,0},{8,12},{12,8},{16,20},{20,16},{24,28},{28,24},{1,5},{5... | collective-permute-start | bytes 7077896 | tf_op jit(solution)/shard_map/ppermute | solution.py:30
  221.0 8.3 %collective-permute-start.37 = (bf16[4,2,24,768]{3,2,1,0:T(8,128)(2,1)S(1)}, bf16[4,2,24,768]{3,2,1,0:T(8,128)(2,1)S(1)}, u32[]{:S(2)}, u32[]{:S(2)}) collective-permute-start(bf16[4,2,24,768]{3,2,1,0:T(8,128)(2,1)S(1)} %fusion.74), channel_id=1, source_target_pairs={{0,8},{4,12},{8,0},{12,4},{16,24},{20,28},{24,16},{28,20},{1,9},{5... | collective-permute-start | bytes 884744 | tf_op jit(solution)/shard_map/ppermute | solution.py:30
  225.9 63.0 %collective-permute-start.27 = (bf16[4,2,2,96,576]{4,3,2,1,0:T(8,128)(2,1)}, bf16[4,2,2,96,576]{4,3,2,1,0:T(8,128)(2,1)}, u32[]{:S(2)}, u32[]{:S(2)}) collective-permute-start(bf16[4,2,2,96,576]{4,3,2,1,0:T(8,128)(2,1)} %fusion.13), channel_id=1, source_target_pairs={{0,4},{4,0},{8,12},{12,8},{16,20},{20,16},{24,28},{28,24},{1,5},{5... | collective-permute-start | bytes 5308424 | tf_op jit(solution)/shard_map/ppermute | solution.py:30
  233.5 48.5 %collective-permute-start.41 = (bf16[24,768]{1,0:T(8,128)(2,1)S(1)}, bf16[24,768]{1,0:T(8,128)(2,1)S(1)}, u32[]{:S(2)}, u32[]{:S(2)}) collective-permute-start(bf16[24,768]{1,0:T(8,128)(2,1)S(1)} %get-tuple-element.154), channel_id=1, source_target_pairs={{0,1},{1,2},{2,3},{3,0},{4,5},{5,6},{6,7},{7,4},{8,9},{9,10},{10,1... | collective-permute-start | bytes 110600 | tf_op jit(solution)/shard_map/ppermute | solution.py:34
  235.7 47.8 %collective-permute-start.40 = (bf16[24,768]{1,0:T(8,128)(2,1)S(1)}, bf16[24,768]{1,0:T(8,128)(2,1)S(1)}, u32[]{:S(2)}, u32[]{:S(2)}) collective-permute-start(bf16[24,768]{1,0:T(8,128)(2,1)S(1)} %get-tuple-element.155), channel_id=1, source_target_pairs={{0,2},{1,3},{2,0},{3,1},{4,6},{5,7},{6,4},{7,5},{8,10},{9,11},{10,... | collective-permute-start | bytes 110600 | tf_op jit(solution)/shard_map/ppermute | solution.py:34
  240.3 43.3 %collective-permute-start.39 = (bf16[24,768]{1,0:T(8,128)(2,1)S(1)}, bf16[24,768]{1,0:T(8,128)(2,1)S(1)}, u32[]{:S(2)}, u32[]{:S(2)}) collective-permute-start(bf16[24,768]{1,0:T(8,128)(2,1)S(1)} %get-tuple-element.153), channel_id=1, source_target_pairs={{0,3},{1,0},{2,1},{3,2},{4,7},{5,4},{6,5},{7,6},{8,11},{9,8},{10,9... | collective-permute-start | bytes 110600 | tf_op jit(solution)/shard_map/ppermute | solution.py:34
  282.0 33.6 %collective-permute-start.54 = (bf16[4,2,2,96,768]{4,3,0,2,1:T(8,128)(2,1)}, bf16[4,2,2,96,768]{4,3,0,2,1:T(8,128)(2,1)S(1)}, u32[]{:S(2)}, u32[]{:S(2)}) collective-permute-start(bf16[4,2,2,96,768]{4,3,0,2,1:T(8,128)(2,1)} %fusion.9), channel_id=1, source_target_pairs={{0,4},{4,0},{8,12},{12,8},{16,20},{20,16},{24,28},{28,24},{1,5},{5... | collective-permute-start | bytes 7077896 | tf_op jit(solution)/shard_map/ppermute | solution.py:30
  292.2 22.3 %collective-permute-start.28 = (bf16[4,2,96,576]{3,2,1,0:T(8,128)(2,1)S(1)}, bf16[4,2,96,576]{3,2,1,0:T(8,128)(2,1)S(1)}, u32[]{:S(2)}, u32[]{:S(2)}) collective-permute-start(bf16[4,2,96,576]{3,2,1,0:T(8,128)(2,1)S(1)} %fusion.43), channel_id=1, source_target_pairs={{0,16},{4,20},{8,24},{12,28},{16,0},{20,4},{24,8},{28,12},{1,17},{... | collective-permute-start | bytes 2654216 | tf_op jit(solution)/shard_map/ppermute | solution.py:30
  314.8 10.9 %collective-permute-start.29 = (bf16[4,96,576]{2,1,0:T(8,128)(2,1)S(1)}, bf16[4,96,576]{2,1,0:T(8,128)(2,1)S(1)}, u32[]{:S(2)}, u32[]{:S(2)}) collective-permute-start(bf16[4,96,576]{2,1,0:T(8,128)(2,1)S(1)} %fusion.72), channel_id=1, source_target_pairs={{0,8},{4,12},{8,0},{12,4},{16,24},{20,28},{24,16},{28,20},{1,9},{5... | collective-permute-start | bytes 1327112 | tf_op jit(solution)/shard_map/ppermute | solution.py:30
  315.5 40.8 %collective-permute-start.46 = (bf16[4,2,96,768]{3,2,0,1:T(8,128)(2,1)S(1)}, bf16[4,2,96,768]{3,2,0,1:T(8,128)(2,1)S(1)}, u32[]{:S(2)}, u32[]{:S(2)}) collective-permute-start(bf16[4,2,96,768]{3,2,0,1:T(8,128)(2,1)S(1)} %fusion.40), channel_id=1, source_target_pairs={{0,16},{4,20},{8,24},{12,28},{16,0},{20,4},{24,8},{28,12},{1,17},{... | collective-permute-start | bytes 3538952 | tf_op jit(solution)/shard_map/ppermute | solution.py:30
  325.9 8.1 %collective-permute-start.31 = (bf16[96,576]{1,0:T(8,128)(2,1)S(1)}, bf16[96,576]{1,0:T(8,128)(2,1)S(1)}, u32[]{:S(2)}, u32[]{:S(2)}) collective-permute-start(bf16[96,576]{1,0:T(8,128)(2,1)S(1)} %get-tuple-element.140), channel_id=1, source_target_pairs={{0,2},{1,3},{2,0},{3,1},{4,6},{5,7},{6,4},{7,5},{8,10},{9,11},{10,... | collective-permute-start | bytes 331784 | tf_op jit(solution)/shard_map/ppermute | solution.py:34
  329.3 28.7 %collective-permute-start.55 = (bf16[4,2,96,768]{3,2,0,1:T(8,128)(2,1)S(1)}, bf16[4,2,96,768]{3,2,0,1:T(8,128)(2,1)S(1)}, u32[]{:S(2)}, u32[]{:S(2)}) collective-permute-start(bf16[4,2,96,768]{3,2,0,1:T(8,128)(2,1)S(1)} %fusion.41), channel_id=1, source_target_pairs={{0,8},{4,12},{8,0},{12,4},{16,24},{20,28},{24,16},{28,20},{1,9},{5... | collective-permute-start | bytes 3538952 | tf_op jit(solution)/shard_map/ppermute | solution.py:30
  334.0 22.0 %collective-permute-start.33 = (bf16[96,576]{1,0:T(8,128)(2,1)S(1)}, bf16[96,576]{1,0:T(8,128)(2,1)S(1)}, u32[]{:S(2)}, u32[]{:S(2)}) collective-permute-start(bf16[96,576]{1,0:T(8,128)(2,1)S(1)} %fusion.86), channel_id=1, source_target_pairs={{0,8},{4,12},{8,0},{12,4},{16,24},{20,28},{24,16},{28,20},{1,9},{5... | collective-permute-start | bytes 331784 | tf_op jit(solution)/shard_map/ppermute | solution.py:30
  356.7 13.5 %collective-permute-start.47 = (bf16[4,96,768]{2,1,0:T(8,128)(2,1)S(1)}, bf16[4,96,768]{2,1,0:T(8,128)(2,1)S(1)}, u32[]{:S(2)}, u32[]{:S(2)}) collective-permute-start(bf16[4,96,768]{2,1,0:T(8,128)(2,1)S(1)} %fusion.69), channel_id=1, source_target_pairs={{0,8},{4,12},{8,0},{12,4},{16,24},{20,28},{24,16},{28,20},{1,9},{5... | collective-permute-start | bytes 1769480 | tf_op jit(solution)/shard_map/ppermute | solution.py:30
  358.3 16.3 %collective-permute-start.56 = (bf16[4,96,768]{2,1,0:T(8,128)(2,1)S(1)}, bf16[4,96,768]{2,1,0:T(8,128)(2,1)S(1)}, u32[]{:S(2)}, u32[]{:S(2)}) collective-permute-start(bf16[4,96,768]{2,1,0:T(8,128)(2,1)S(1)} %fusion.70), channel_id=1, source_target_pairs={{0,16},{4,20},{8,24},{12,28},{16,0},{20,4},{24,8},{28,12},{1,17},{... | collective-permute-start | bytes 1769480 | tf_op jit(solution)/shard_map/ppermute | solution.py:30
  361.4 13.4 %collective-permute-start.35 = (bf16[2,2,96,576]{3,2,1,0:T(8,128)(2,1)S(1)}, bf16[2,2,96,576]{3,2,1,0:T(8,128)(2,1)S(1)}, u32[]{:S(2)}, u32[]{:S(2)}) collective-permute-start(bf16[2,2,96,576]{3,2,1,0:T(8,128)(2,1)S(1)} %maximum_select_fusion.24), channel_id=1, source_target_pairs={{0,4},{4,0},{8,12},{12,8},{16,20},{20,16},{24,28},{28,24},{1,5},{5... | collective-permute-start | bytes 1327112 | tf_op jit(solution)/shard_map/ppermute | solution.py:30
  370.7 14.3 %collective-permute-start.49 = (bf16[96,768]{1,0:T(8,128)(2,1)S(1)}, bf16[96,768]{1,0:T(8,128)(2,1)S(1)}, u32[]{:S(2)}, u32[]{:S(2)}) collective-permute-start(bf16[96,768]{1,0:T(8,128)(2,1)S(1)} %get-tuple-element.137), channel_id=1, source_target_pairs={{0,2},{1,3},{2,0},{3,1},{4,6},{5,7},{6,4},{7,5},{8,10},{9,11},{10,... | collective-permute-start | bytes 442376 | tf_op jit(solution)/shard_map/ppermute | solution.py:34
  372.2 12.7 %collective-permute-start.48 = (bf16[96,768]{1,0:T(8,128)(2,1)S(1)}, bf16[96,768]{1,0:T(8,128)(2,1)S(1)}, u32[]{:S(2)}, u32[]{:S(2)}) collective-permute-start(bf16[96,768]{1,0:T(8,128)(2,1)S(1)} %get-tuple-element.135), channel_id=1, source_target_pairs={{0,3},{1,0},{2,1},{3,2},{4,7},{5,4},{6,5},{7,6},{8,11},{9,8},{10,9... | collective-permute-start | bytes 442376 | tf_op jit(solution)/shard_map/ppermute | solution.py:34
  374.7 11.2 %collective-permute-start.59 = (bf16[96,768]{1,0:T(8,128)(2,1)S(1)}, bf16[96,768]{1,0:T(8,128)(2,1)S(1)}, u32[]{:S(2)}, u32[]{:S(2)}) collective-permute-start(bf16[96,768]{1,0:T(8,128)(2,1)S(1)} %get-tuple-element.133), channel_id=1, source_target_pairs={{0,1},{1,2},{2,3},{3,0},{4,5},{5,6},{6,7},{7,4},{8,9},{9,10},{10,1... | collective-permute-start | bytes 442376 | tf_op jit(solution)/shard_map/ppermute | solution.py:34
  374.8 20.9 %collective-permute-start.58 = (bf16[96,768]{1,0:T(8,128)(2,1)S(1)}, bf16[96,768]{1,0:T(8,128)(2,1)S(1)}, u32[]{:S(2)}, u32[]{:S(2)}) collective-permute-start(bf16[96,768]{1,0:T(8,128)(2,1)S(1)} %get-tuple-element.134), channel_id=1, source_target_pairs={{0,2},{1,3},{2,0},{3,1},{4,6},{5,7},{6,4},{7,5},{8,10},{9,11},{10,... | collective-permute-start | bytes 442376 | tf_op jit(solution)/shard_map/ppermute | solution.py:34
  376.4 19.3 %collective-permute-start.57 = (bf16[96,768]{1,0:T(8,128)(2,1)S(1)}, bf16[96,768]{1,0:T(8,128)(2,1)S(1)}, u32[]{:S(2)}, u32[]{:S(2)}) collective-permute-start(bf16[96,768]{1,0:T(8,128)(2,1)S(1)} %get-tuple-element.132), channel_id=1, source_target_pairs={{0,3},{1,0},{2,1},{3,2},{4,7},{5,4},{6,5},{7,6},{8,11},{9,8},{10,9... | collective-permute-start | bytes 442376 | tf_op jit(solution)/shard_map/ppermute | solution.py:34
  385.1 13.0 %collective-permute-start.51 = (bf16[96,768]{1,0:T(8,128)(2,1)S(1)}, bf16[96,768]{1,0:T(8,128)(2,1)S(1)}, u32[]{:S(2)}, u32[]{:S(2)}) collective-permute-start(bf16[96,768]{1,0:T(8,128)(2,1)S(1)} %fusion.82), channel_id=1, source_target_pairs={{0,8},{4,12},{8,0},{12,4},{16,24},{20,28},{24,16},{28,20},{1,9},{5... | collective-permute-start | bytes 442376 | tf_op jit(solution)/shard_map/ppermute | solution.py:30
  398.1 9.0 %collective-permute-start.52 = (bf16[2,96,768]{2,1,0:T(8,128)(2,1)S(1)}, bf16[2,96,768]{2,1,0:T(8,128)(2,1)S(1)}, u32[]{:S(2)}, u32[]{:S(2)}) collective-permute-start(bf16[2,96,768]{2,1,0:T(8,128)(2,1)S(1)} %maximum_select_fusion.27), channel_id=1, source_target_pairs={{0,16},{4,20},{8,24},{12,28},{16,0},{20,4},{24,8},{28,12},{1,17},{... | collective-permute-start | bytes 884744 | tf_op jit(solution)/shard_map/ppermute | solution.py:30
  399.9 9.5 %collective-permute-start.61 = (bf16[2,96,768]{2,1,0:T(8,128)(2,1)S(1)}, bf16[2,96,768]{2,1,0:T(8,128)(2,1)S(1)}, u32[]{:S(2)}, u32[]{:S(2)}) collective-permute-start(bf16[2,96,768]{2,1,0:T(8,128)(2,1)S(1)} %maximum_select_fusion.29), channel_id=1, source_target_pairs={{0,8},{4,12},{8,0},{12,4},{16,24},{20,28},{24,16},{28,20},{1,9},{5... | collective-permute-start | bytes 884744 | tf_op jit(solution)/shard_map/ppermute | solution.py:30
  (44 other events, 368.1 us)
where the time goes:
time: 421 us; the launch traced here: 416 us
  waiting for transfers between devices  123 us (29%)
  starting transfers between devices  92.6 us (22%)
  matrix products  68.3 us (16%)
  other arithmetic  44.1 us (10%)
  blocking collectives  41.7 us (10%)
  local copies, waits for them, and re-layouts  39.2 us (9%)
  between operations  7.74 us (2%)
    ppermute x36, waiting for transfers between devices, swap(): lax.ppermute(value, 'dp', [(d, d ^ 1 << which) for d in range(self.dp)])  92 us
    ppermute x36, starting transfers between devices, swap(): lax.ppermute(value, 'dp', [(d, d ^ 1 << which) for d in range(self.dp)])  45.5 us
    psum x1, blocking collectives, on_device(): lax.psum(jnp.concatenate([shared, split.reshape(-1)]), ('dp', 'tensor'))  41.7 us
    ppermute x21, starting transfers between devices, turn(): lax.ppermute(value, 'tensor', [(k, (k + step) % size) for k in range(size)])  35.5 us
    ppermute x21, waiting for transfers between devices, turn(): lax.ppermute(value, 'tensor', [(k, (k + step) % size) for k in range(size)])  30.6 us
    ppermute x6, starting transfers between devices, onward(): return lax.ppermute(value, 'tensor', pairs)  11.5 us
    convert_element_type x12, local copies, waits for them, and re-layouts, keep_and_send(): return (kept.astype(F32), sent.astype(BF16))  11 us
    add x8, other arithmetic, reduce_pieces(): value = kept + places.swap(sent, which).astype(F32)  9.47 us
  transfers between devices with their start and end apart: 63, of which 22 were waited for; matrix products, arithmetic and copies ran while one was open for 26% of the time, Pallas kernels for 0%

commit v1 on v0

--- a/solution.py
+++ b/solution.py
@@ -294,7 +294,9 @@
     split = jnp.concatenate([d_b_qkv, d_b_in], axis=1)
     turned = jnp.concatenate([split[::-1], split[::-1]])
     split = lax.dynamic_slice_in_dim(turned, tensor - 1 - places.z, tensor, 0)
-    summed = lax.psum(jnp.concatenate([shared, split.reshape(-1)]), ("dp", "tensor"))
+    summed = jnp.sum(
+        lax.all_gather(jnp.concatenate([shared, split.reshape(-1)]), ("dp", "tensor")), axis=0
+    )
     d_b_out, d_gain_one, d_shift_one, d_b_two, d_gain_two, d_shift_two = jnp.split(
         summed[: 6 * width], 6
     )

time: 421 us -> 399 us (0.948)
  blocking collectives: 41.7 us -> 0 us
  between operations: 7.74 us -> 21.3 us
  starting transfers between devices: 92.6 us -> 98.2 us
    psum x1 -> x0, blocking collectives: 41.7 us -> none  [on_device(): lax.psum(jnp.concatenate([shared, split.reshape(-1)]), ('dp', 'tensor'))]
    ppermute x36, starting transfers between devices: 45.5 us -> 54.6 us  [swap(): lax.ppermute(value, 'dp', [(d, d ^ 1 << which) for d in range(self.dp)])]
    slice x10, local copies, waits for them, and re-layouts: 4.64 us -> 0.12 us  [shift_shards(): return jnp.roll(state, step, axis=0)]
    dot_general x1, matrix products: 5.21 us -> 9.44 us  [on_device(): g_two = jnp.einsum('td,jtc->jdc', d_second, act, preferred_element_type=F32)]
    unnamed x68 -> x65, local copies, waits for them, and re-layouts: 8.69 us -> 9.05 us
  transfers between devices with their start and end apart: 63 -> 64, of which waited for: 22 -> 27; matrix products, arithmetic and copies ran while one was open for 26% -> 28% of each run, Pallas kernels for 0% -> 0%
where the time goes in v1:
time: 399 us; the launch traced here: 394 us
  waiting for transfers between devices  122 us (31%)
  starting transfers between devices  98.2 us (25%)
  matrix products  67.5 us (17%)
  other arithmetic  48 us (12%)
  local copies, waits for them, and re-layouts  37.4 us (9%)
  between operations  21.3 us (5%)
    ppermute x36, waiting for transfers between devices, swap(): lax.ppermute(value, 'dp', [(d, d ^ 1 << which) for d in range(self.dp)])  92.3 us
    ppermute x36, starting transfers between devices, swap(): lax.ppermute(value, 'dp', [(d, d ^ 1 << which) for d in range(self.dp)])  54.6 us
    ppermute x21, starting transfers between devices, turn(): lax.ppermute(value, 'tensor', [(k, (k + step) % size) for k in range(size)])  33.9 us
    ppermute x21, waiting for transfers between devices, turn(): lax.ppermute(value, 'tensor', [(k, (k + step) % size) for k in range(size)])  27.9 us
    convert_element_type x12, local copies, waits for them, and re-layouts, keep_and_send(): return (kept.astype(F32), sent.astype(BF16))  13.4 us
    add x8, other arithmetic, reduce_pieces(): value = kept + places.swap(sent, which).astype(F32)  12 us
    ppermute x6, starting transfers between devices, onward(): return lax.ppermute(value, 'tensor', pairs)  9.58 us
    dot_general x1, matrix products, on_device(): g_two = jnp.einsum('td,jtc->jdc', d_second, act, preferred_element_type=F32)  9.44 us
  transfers between devices with their start and end apart: 64, of which 27 were waited for; matrix products, arithmetic and copies ran while one was open for 28% of the time, Pallas kernels for 0%

profile of v1, /device:TPU:1, one launch (start us, length us, event | category | flops | bytes accessed | tf_op | source)
XLA Modules:
  0.0 394.0 jit_solution(11147364953550880399)
XLA Ops:
  9.2 4.2 %collective-permute-start.20 = (bf16[216,768]{1,0:T(8,128)(2,1)S(1)}, bf16[216,768]{1,0:T(8,128)(2,1)S(1)}, u32[]{:S(2)}, u32[]{:S(2)}) collective-permute-start(bf16[216,768]{1,0:T(8,128)(2,1)S(1)} %get-tuple-element.142), channel_id=1, source_target_pairs={{0,3},{1,0},{2,1},{3,2},{4,7},{5,4},{6,5},{7,6},{8,11},{9,8},{10,9... | collective-permute-start | bytes 995336 | tf_op jit(solution)/shard_map/ppermute | solution.py:34
  14.5 2.3 collective-permute-start.10
  21.1 2.3 cosine_select_fusion
  29.9 4.4 %collective-permute-start.15 = (bf16[216,768]{1,0:T(8,128)(2,1)S(1)}, bf16[216,768]{1,0:T(8,128)(2,1)S(1)}, u32[]{:S(2)}, u32[]{:S(2)}) collective-permute-start(bf16[216,768]{1,0:T(8,128)(2,1)S(1)} %get-tuple-element.142), channel_id=1, source_target_pairs={{0,1},{1,2},{2,3},{3,0},{4,5},{5,6},{6,7},{7,4},{8,9},{9,10},{10,1... | collective-permute-start | bytes 995336 | tf_op jit(solution)/shard_map/ppermute | solution.py:34
  34.5 3.6 collective-permute-start.5
  38.2 5.2 %collective-permute-done.5 = bf16[96,576]{1,0:T(8,128)(2,1)S(1)} collective-permute-done((bf16[96,576]{1,0:T(8,128)(2,1)S(1)}, bf16[96,576]{1,0:T(8,128)(2,1)S(1)}, u32[]{:S(2)}, u32[]{:S(2)}) %collective-permute-start.5) | collective-permute-done | bytes 110624 | tf_op jit(solution)/shard_map/ppermute | solution.py:34
  43.5 2.2 collective-permute-start
  47.8 2.3 collective-permute-done
  57.3 15.7 %collective-permute-done.7 = bf16[2,2,96,576]{3,2,1,0:T(8,128)(2,1)S(1)} collective-permute-done((bf16[2,2,96,576]{3,2,1,0:T(8,128)(2,1)S(1)}, bf16[2,2,96,576]{3,2,1,0:T(8,128)(2,1)S(1)}, u32[]{:S(2)}, u32[]{:S(2)}) %collective-permute-start.7) | collective-permute-done | bytes 442400 | tf_op jit(solution)/shard_map/ppermute | solution.py:30
  73.2 10.8 %collective-permute-start.8 = (bf16[2,2,2,96,576]{4,3,2,1,0:T(8,128)(2,1)S(1)}, bf16[2,2,2,96,576]{4,3,2,1,0:T(8,128)(2,1)S(1)}, u32[]{:S(2)}, u32[]{:S(2)}) collective-permute-start(bf16[2,2,2,96,576]{4,3,2,1,0:T(8,128)(2,1)S(1)} %maximum_select_fusion.14), channel_id=1, source_target_pairs={{0,4},{4,0},{8,12},{12,8},{16,20},{20,16},{24,28},{28,24},{1,5},{5... | collective-permute-start | bytes 2654216 | tf_op jit(solution)/shard_map/ppermute | solution.py:30
  91.4 2.5 broadcast_add_fusion
  95.3 2.3 collective-permute-start.12
  105.0 10.5 %collective-permute-done.22 = bf16[2,2,216,768]{3,2,0,1:T(8,128)(2,1)S(1)} collective-permute-done((bf16[2,2,216,768]{3,2,0,1:T(8,128)(2,1)S(1)}, bf16[2,2,216,768]{3,2,0,1:T(8,128)(2,1)S(1)}, u32[]{:S(2)}, u32[]{:S(2)}) %collective-permute-start.22) | collective-permute-done | bytes 1327136 | tf_op jit(solution)/shard_map/ppermute | solution.py:30
  115.4 2.1 maximum_select_fusion.4
  123.8 3.4 fusion.7
  127.5 3.0 pad_maximum_fusion.1
  131.8 4.8 %fusion.56 = f32[4,768,512]{1,2,0:T(8,128)} fusion(bf16[4,768,768]{2,1,0:T(8,128)(2,1)S(1)} %bitcast.427, f32[512,768]{1,0:T(8,128)S(1)} %get-tuple-element.171, f32[768]{0:T(1024)S(1)} %convert_element_type.549, f32[768]{0:T(1024)S(1)} %convert_element_type.548, f32[512]{0:T(512)S(1)} %add_rsqrt_fusion.1, f32[512]{0:T(512)S(1)} %broadcast_multiply_fusion.5), kind=kOutput, calls=%fused_computation.163 | convolution fusion | flops 2417885184 | bytes 12593152 | tf_op jit(solution)/shard_map/td,jdc->jtc/dot_general | solution.py:227
  136.7 6.3 %fusion.145 = (f32[512]{0:T(512)S(1)}, f32[512,768]{1,0:T(8,128)S(1)}) fusion(f32[768]{0:T(1024)S(1)} %convert_element_type.554, bf16[4,768,768]{2,1,0:T(8,128)(2,1)S(1)} %bitcast.431, f32[4,768,512]{1,2,0:T(8,128)} %fusion.56, f32[4,768]{1,0:T(4,128)S(1)} %fusion.96, f32[768]{0:T(1024)S(1)} %convert_element_type.549, f32[768]{0:T(1024)S(1)} %convert_element_type.548, ...), kind=kOutput, calls=%fused_computation.357 | convolution fusion | flops 2435186176 | bytes 14183424 | tf_op jit(solution)/shard_map/jtc,jcd->td/dot_general | solution.py:230
  146.5 9.1 %convert_reduce_fusion = (f32[4,768]{1,0:T(4,128)S(1)}, bf16[4,512,768]{2,1,0:T(8,128)(2,1)}) fusion(f32[4,768,512]{1,2,0:T(8,128)} %fusion.56, f32[4,768]{1,0:T(4,128)S(1)} %fusion.96, bf16[4,768,768]{2,1,0:T(8,128)(2,1)S(1)} %bitcast.432, f32[512,768]{1,0:T(8,128)S(1)} %get-tuple-element.97), kind=kOutput, calls=%fused_computation.12 | convolution fusion | flops 2450912256 | bytes 15753216 | tf_op jit(solution)/shard_map/td,jcd->jtc/dot_general | solution.py:239
  155.6 5.0 %multiply_reduce_fusion = (f32[768]{0:T(1024)S(1)}, f32[512]{0:T(512)S(1)}, f32[512]{0:T(512)S(1)}, f32[768]{0:T(1024)S(1)}, f32[512,768]{1,0:T(8,128)S(1)}) fusion(f32[512,768]{1,0:T(8,128)S(1)} %get-tuple-element.171, f32[512]{0:T(512)S(1)} %add_rsqrt_fusion.1, f32[512]{0:T(512)S(1)} %broadcast_multiply_fusion.5, f32[768]{0:T(1024)S(1)} %convert_element_type.548, ...), kind=kOutput, calls=%fused_computation.99 | convolution fusion | flops 2419848704 | bytes 12600320 | tf_op jit(solution)/shard_map/jtc,jdc->td/dot_general | solution.py:244
  170.2 5.5 %fusion.54 = f32[4,768,768]{1,2,0:T(8,128)} fusion(bf16[4,512,768]{2,1,0:T(8,128)(2,1)S(1)} %copy-done.21, f32[512,768]{1,0:T(8,128)S(1)} %get-tuple-element.171, f32[768]{0:T(1024)S(1)} %convert_element_type.549, f32[768]{0:T(1024)S(1)} %convert_element_type.548, f32[512]{0:T(512)S(1)} %add_rsqrt_fusion.1, f32[512]{0:T(512)S(1)} %broadcast_multiply_fusion.5), kind=kOutput, calls=%fused_computation.161 | convolution fusion | flops 2417885184 | bytes 14166016 | tf_op jit(solution)/shard_map/td,jtc->jdc/dot_general | solution.py:242
  175.7 9.4 %fusion.51 = f32[4,768,768]{1,2,0:T(8,128)} fusion(f32[512,768]{1,0:T(8,128)S(1)} %get-tuple-element.97, f32[4,768,512]{1,2,0:T(8,128)} %fusion.56, f32[4,768]{1,0:T(4,128)S(1)} %fusion.96), kind=kOutput, calls=%fused_computation.158 | convolution fusion | flops 2432040960 | bytes 17313792 | tf_op jit(solution)/shard_map/td,jtc->jdc/dot_general | solution.py:236
  187.1 4.0 %fusion.8 = bf16[4,2,2,96,768]{4,3,0,2,1:T(8,128)(2,1)} fusion(f32[4,2,2,2,96,768]{5,4,3,2,1,0:T(8,128)} %bitcast.421, s32[]{:T(128)S(6)} %select_n.542), kind=kLoop, calls=%fused_computation.37 | loop fusion | bytes 4718596 | tf_op jit(solution)/shard_map/convert_element_type | solution.py:73
  193.4 4.0 %fusion.9 = bf16[4,2,2,96,768]{4,3,0,2,1:T(8,128)(2,1)} fusion(f32[4,2,2,2,96,768]{5,4,3,2,1,0:T(8,128)} %bitcast.417, s32[]{:T(128)S(6)} %select_n.542), kind=kLoop, calls=%fused_computation.38 | loop fusion | bytes 4718596 | tf_op jit(solution)/shard_map/convert_element_type | solution.py:73
  203.3 3.2 fusion.33
  207.8 5.2 %convolution_bitcast_fusion = f32[4,768,576]{1,2,0:T(8,128)} fusion(bf16[4,512,576]{1,2,0:T(8,128)(2,1)S(1)} %bitcast.413, bf16[512,768]{1,0:T(8,128)(2,1)S(1)} %copy-done.13), kind=kOutput, calls=%fused_computation.27 | convolution fusion | flops 1811939328 | bytes 10223616 | tf_op jit(solution)/shard_map/td,jtc->jdc/dot_general | solution.py:288
  213.0 8.4 %copy.194 = f32[4,768,576]{2,1,0:T(8,128)} copy(f32[4,768,576]{1,2,0:T(8,128)} %convolution_bitcast_fusion) | data formatting | bytes 14155776 | tf_op jit(solution)/shard_map/td,jtc->jdc/transpose | solution.py:288
  221.4 3.7 fusion.13
  227.6 3.9 collective-permute-done.38
  233.3 3.9 collective-permute-start.40
  244.3 2.7 collective-permute-done.43
  246.9 4.2 %collective-permute-start.44 = (bf16[2,2,24,768]{3,2,1,0:T(8,128)(2,1)S(1)}, bf16[2,2,24,768]{3,2,1,0:T(8,128)(2,1)S(1)}, u32[]{:S(2)}, u32[]{:S(2)}) collective-permute-start(bf16[2,2,24,768]{3,2,1,0:T(8,128)(2,1)S(1)} %maximum_select_fusion.33), channel_id=1, source_target_pairs={{0,4},{4,0},{8,12},{12,8},{16,20},{20,16},{24,28},{28,24},{1,5},{5... | collective-permute-start | bytes 442376 | tf_op jit(solution)/shard_map/ppermute | solution.py:30
  251.1 3.1 bitcast_add_fusion.2
  256.6 3.7 bitcast_add_fusion.1
  260.4 18.1 %collective-permute-done.28 = bf16[4,2,96,576]{3,2,1,0:T(8,128)(2,1)S(1)} collective-permute-done((bf16[4,2,96,576]{3,2,1,0:T(8,128)(2,1)S(1)}, bf16[4,2,96,576]{3,2,1,0:T(8,128)(2,1)S(1)}, u32[]{:S(2)}, u32[]{:S(2)}) %collective-permute-start.28) | collective-permute-done | bytes 884768 | tf_op jit(solution)/shard_map/ppermute | solution.py:30
  282.6 10.7 %collective-permute-done.29 = bf16[4,96,576]{2,1,0:T(8,128)(2,1)S(1)} collective-permute-done((bf16[4,96,576]{2,1,0:T(8,128)(2,1)S(1)}, bf16[4,96,576]{2,1,0:T(8,128)(2,1)S(1)}, u32[]{:S(2)}, u32[]{:S(2)}) %collective-permute-start.29) | collective-permute-done | bytes 442400 | tf_op jit(solution)/shard_map/ppermute | solution.py:30
  293.5 2.2 collective-permute-start.31
  299.0 2.0 reduce_sum.292
  306.4 18.6 %collective-permute-done.33 = bf16[96,576]{1,0:T(8,128)(2,1)S(1)} collective-permute-done((bf16[96,576]{1,0:T(8,128)(2,1)S(1)}, bf16[96,576]{1,0:T(8,128)(2,1)S(1)}, u32[]{:S(2)}, u32[]{:S(2)}) %collective-permute-start.33) | collective-permute-done | bytes 110624 | tf_op jit(solution)/shard_map/ppermute | solution.py:30
  326.5 2.5 bitcast_add_fusion.4
  332.1 3.6 collective-permute-start.35
  335.8 4.9 %collective-permute-done.47 = bf16[4,96,768]{2,1,0:T(8,128)(2,1)S(1)} collective-permute-done((bf16[4,96,768]{2,1,0:T(8,128)(2,1)S(1)}, bf16[4,96,768]{2,1,0:T(8,128)(2,1)S(1)}, u32[]{:S(2)}, u32[]{:S(2)}) %collective-permute-start.47) | collective-permute-done | bytes 589856 | tf_op jit(solution)/shard_map/ppermute | solution.py:30
  342.1 2.3 collective-permute-start.48
  350.0 3.4 collective-permute-done.59
  353.4 11.2 %collective-permute-done.58 = bf16[96,768]{1,0:T(8,128)(2,1)S(1)} collective-permute-done((bf16[96,768]{1,0:T(8,128)(2,1)S(1)}, bf16[96,768]{1,0:T(8,128)(2,1)S(1)}, u32[]{:S(2)}, u32[]{:S(2)}) %collective-permute-start.58) | collective-permute-done | bytes 147488 | tf_op jit(solution)/shard_map/ppermute | solution.py:34
  369.7 4.6 %collective-permute-done.52 = bf16[2,96,768]{2,1,0:T(8,128)(2,1)S(1)} collective-permute-done((bf16[2,96,768]{2,1,0:T(8,128)(2,1)S(1)}, bf16[2,96,768]{2,1,0:T(8,128)(2,1)S(1)}, u32[]{:S(2)}, u32[]{:S(2)}) %collective-permute-start.52) | collective-permute-done | bytes 294944 | tf_op jit(solution)/shard_map/ppermute | solution.py:30
  374.4 4.3 %collective-permute-start.53 = (bf16[2,2,96,768]{3,2,1,0:T(8,128)(2,1)S(1)}, bf16[2,2,96,768]{3,2,1,0:T(8,128)(2,1)S(1)}, u32[]{:S(2)}, u32[]{:S(2)}) collective-permute-start(bf16[2,2,96,768]{3,2,1,0:T(8,128)(2,1)S(1)} %maximum_select_fusion.17), channel_id=1, source_target_pairs={{0,4},{4,0},{8,12},{12,8},{16,20},{20,16},{24,28},{28,24},{1,5},{5... | collective-permute-start | bytes 1769480 | tf_op jit(solution)/shard_map/ppermute | solution.py:30
  378.8 3.3 collective-permute-start.62
  (343 shorter events, 114.0 us)
Async XLA Ops:
  7.3 291.7 %all-gather.4.cloned.1.call-start = ((), (), s32[]{:S(2)}) async-start(), calls=%async_computation | async-start | bytes 1317888 | tf_op jit(solution)/shard_map/all_gather | solution.py:298
  9.2 42.3 %collective-permute-start.20 = (bf16[216,768]{1,0:T(8,128)(2,1)S(1)}, bf16[216,768]{1,0:T(8,128)(2,1)S(1)}, u32[]{:S(2)}, u32[]{:S(2)}) collective-permute-start(bf16[216,768]{1,0:T(8,128)(2,1)S(1)} %get-tuple-element.142), channel_id=1, source_target_pairs={{0,3},{1,0},{2,1},{3,2},{4,7},{5,4},{6,5},{7,6},{8,11},{9,8},{10,9... | collective-permute-start | bytes 995336 | tf_op jit(solution)/shard_map/ppermute | solution.py:34
  13.4 38.1 %collective-permute-start.19 = (bf16[216,768]{1,0:T(8,128)(2,1)S(1)}, bf16[216,768]{1,0:T(8,128)(2,1)S(1)}, u32[]{:S(2)}, u32[]{:S(2)}) collective-permute-start(bf16[216,768]{1,0:T(8,128)(2,1)S(1)} %get-tuple-element.142), channel_id=1, source_target_pairs={{0,2},{1,3},{2,0},{3,1},{4,6},{5,7},{6,4},{7,5},{8,10},{9,11},{10,... | collective-permute-start | bytes 995336 | tf_op jit(solution)/shard_map/ppermute | solution.py:34
  14.2 15.7 %collective-permute-start.11 = (bf16[1,1344]{1,0:T(2,128)(2,1)S(1)}, bf16[1,1344]{1,0:T(2,128)(2,1)S(1)}, u32[]{:S(2)}, u32[]{:S(2)}) collective-permute-start(bf16[1,1344]{1,0:T(2,128)(2,1)S(1)} %reshape.1789), channel_id=1, source_target_pairs={{0,3},{1,0},{2,1},{3,2},{4,7},{5,4},{6,5},{7,6},{8,11},{9,8},{10,9... | collective-permute-start | bytes 8072 | tf_op jit(solution)/shard_map/ppermute | solution.py:34
  14.5 20.1 %collective-permute-start.10 = (bf16[1,1344]{1,0:T(2,128)(2,1)S(1)}, bf16[1,1344]{1,0:T(2,128)(2,1)S(1)}, u32[]{:S(2)}, u32[]{:S(2)}) collective-permute-start(bf16[1,1344]{1,0:T(2,128)(2,1)S(1)} %reshape.1789), channel_id=1, source_target_pairs={{0,2},{1,3},{2,0},{3,1},{4,6},{5,7},{6,4},{7,5},{8,10},{9,11},{10,... | collective-permute-start | bytes 8072 | tf_op jit(solution)/shard_map/ppermute | solution.py:34
  16.7 21.4 %collective-permute-start.9 = (bf16[1,1344]{1,0:T(2,128)(2,1)S(1)}, bf16[1,1344]{1,0:T(2,128)(2,1)S(1)}, u32[]{:S(2)}, u32[]{:S(2)}) collective-permute-start(bf16[1,1344]{1,0:T(2,128)(2,1)S(1)} %reshape.1789), channel_id=1, source_target_pairs={{0,1},{1,2},{2,3},{3,0},{4,5},{5,6},{6,7},{7,4},{8,9},{9,10},{10,1... | collective-permute-start | bytes 8072 | tf_op jit(solution)/shard_map/ppermute | solution.py:34
  29.9 23.0 %collective-permute-start.15 = (bf16[216,768]{1,0:T(8,128)(2,1)S(1)}, bf16[216,768]{1,0:T(8,128)(2,1)S(1)}, u32[]{:S(2)}, u32[]{:S(2)}) collective-permute-start(bf16[216,768]{1,0:T(8,128)(2,1)S(1)} %get-tuple-element.142), channel_id=1, source_target_pairs={{0,1},{1,2},{2,3},{3,0},{4,5},{5,6},{6,7},{7,4},{8,9},{9,10},{10,1... | collective-permute-start | bytes 995336 | tf_op jit(solution)/shard_map/ppermute | solution.py:34
  34.5 8.9 %collective-permute-start.5 = (bf16[96,576]{1,0:T(8,128)(2,1)S(1)}, bf16[96,576]{1,0:T(8,128)(2,1)S(1)}, u32[]{:S(2)}, u32[]{:S(2)}) collective-permute-start(bf16[96,576]{1,0:T(8,128)(2,1)S(1)} %copy.217), channel_id=1, source_target_pairs={{0,3},{1,0},{2,1},{3,2},{4,7},{5,4},{6,5},{7,6},{8,11},{9,8},{10,9... | collective-permute-start | bytes 331784 | tf_op jit(solution)/shard_map/ppermute | solution.py:34
  38.1 8.3 %collective-permute-start.4 = (bf16[96,576]{1,0:T(8,128)(2,1)S(1)}, bf16[96,576]{1,0:T(8,128)(2,1)S(1)}, u32[]{:S(2)}, u32[]{:S(2)}) collective-permute-start(bf16[96,576]{1,0:T(8,128)(2,1)S(1)} %copy.217), channel_id=1, source_target_pairs={{0,2},{1,3},{2,0},{3,1},{4,6},{5,7},{6,4},{7,5},{8,10},{9,11},{10,... | collective-permute-start | bytes 331784 | tf_op jit(solution)/shard_map/ppermute | solution.py:34
  51.6 33.3 %collective-permute-start.21 = (bf16[2,216,768]{2,1,0:T(8,128)(2,1)S(1)}, bf16[2,216,768]{2,1,0:T(8,128)(2,1)S(1)}, u32[]{:S(2)}, u32[]{:S(2)}) collective-permute-start(bf16[2,216,768]{2,1,0:T(8,128)(2,1)S(1)} %get-tuple-element.131), channel_id=1, source_target_pairs={{0,16},{4,20},{8,24},{12,28},{16,0},{20,4},{24,8},{28,12},{1,17},{... | collective-permute-start | bytes 1990664 | tf_op jit(solution)/shard_map/ppermute | solution.py:30
  53.1 33.1 %collective-permute-start.16 = (bf16[2,216,768]{2,1,0:T(8,128)(2,1)S(1)}, bf16[2,216,768]{2,1,0:T(8,128)(2,1)S(1)}, u32[]{:S(2)}, u32[]{:S(2)}) collective-permute-start(bf16[2,216,768]{2,1,0:T(8,128)(2,1)S(1)} %get-tuple-element.128), channel_id=1, source_target_pairs={{0,8},{4,12},{8,0},{12,4},{16,24},{20,28},{24,16},{28,20},{1,9},{5... | collective-permute-start | bytes 1990664 | tf_op jit(solution)/shard_map/ppermute | solution.py:30
  53.5 19.4 %collective-permute-start.7 = (bf16[2,2,96,576]{3,2,1,0:T(8,128)(2,1)S(1)}, bf16[2,2,96,576]{3,2,1,0:T(8,128)(2,1)S(1)}, u32[]{:S(2)}, u32[]{:S(2)}) collective-permute-start(bf16[2,2,96,576]{3,2,1,0:T(8,128)(2,1)S(1)} %maximum_select_fusion.22), channel_id=1, source_target_pairs={{0,8},{4,12},{8,0},{12,4},{16,24},{20,28},{24,16},{28,20},{1,9},{5... | collective-permute-start | bytes 1327112 | tf_op jit(solution)/shard_map/ppermute | solution.py:30
  55.5 28.5 %collective-permute-start.2 = (bf16[2,2,96,576]{3,2,1,0:T(8,128)(2,1)S(1)}, bf16[2,2,96,576]{3,2,1,0:T(8,128)(2,1)S(1)}, u32[]{:S(2)}, u32[]{:S(2)}) collective-permute-start(bf16[2,2,96,576]{3,2,1,0:T(8,128)(2,1)S(1)} %maximum_select_fusion.20), channel_id=1, source_target_pairs={{0,16},{4,20},{8,24},{12,28},{16,0},{20,4},{24,8},{28,12},{1,17},{... | collective-permute-start | bytes 1327112 | tf_op jit(solution)/shard_map/ppermute | solution.py:30
  73.2 15.4 %collective-permute-start.8 = (bf16[2,2,2,96,576]{4,3,2,1,0:T(8,128)(2,1)S(1)}, bf16[2,2,2,96,576]{4,3,2,1,0:T(8,128)(2,1)S(1)}, u32[]{:S(2)}, u32[]{:S(2)}) collective-permute-start(bf16[2,2,2,96,576]{4,3,2,1,0:T(8,128)(2,1)S(1)} %maximum_select_fusion.14), channel_id=1, source_target_pairs={{0,4},{4,0},{8,12},{12,8},{16,20},{20,16},{24,28},{28,24},{1,5},{5... | collective-permute-start | bytes 2654216 | tf_op jit(solution)/shard_map/ppermute | solution.py:30
  85.2 30.3 %collective-permute-start.22 = (bf16[2,2,216,768]{3,2,0,1:T(8,128)(2,1)S(1)}, bf16[2,2,216,768]{3,2,0,1:T(8,128)(2,1)S(1)}, u32[]{:S(2)}, u32[]{:S(2)}) collective-permute-start(bf16[2,2,216,768]{3,2,0,1:T(8,128)(2,1)S(1)} %maximum_select_fusion.9), channel_id=1, source_target_pairs={{0,8},{4,12},{8,0},{12,4},{16,24},{20,28},{24,16},{28,20},{1,9},{5... | collective-permute-start | bytes 3981320 | tf_op jit(solution)/shard_map/ppermute | solution.py:30
  86.4 32.7 %collective-permute-start.17 = (bf16[2,2,216,768]{3,2,1,0:T(8,128)(2,1)S(1)}, bf16[2,2,216,768]{3,2,1,0:T(8,128)(2,1)S(1)}, u32[]{:S(2)}, u32[]{:S(2)}) collective-permute-start(bf16[2,2,216,768]{3,2,1,0:T(8,128)(2,1)S(1)} %maximum_select_fusion.8), channel_id=1, source_target_pairs={{0,16},{4,20},{8,24},{12,28},{16,0},{20,4},{24,8},{28,12},{1,17},{... | collective-permute-start | bytes 3981320 | tf_op jit(solution)/shard_map/ppermute | solution.py:30
  95.3 23.7 %collective-permute-start.12 = (bf16[4,3,128,65]{2,3,1,0:T(8,128)(2,1)S(1)}, bf16[4,3,128,65]{2,3,1,0:T(8,128)(2,1)S(1)}, u32[]{:S(2)}, u32[]{:S(2)}) collective-permute-start(bf16[4,3,128,65]{2,3,1,0:T(8,128)(2,1)S(1)} %convolution_convert_fusion.1), channel_id=1, source_target_pairs={{0,1},{1,2},{2,3},{4,5},{5,6},{6,7},{8,9},{9,10},{10,11},{12,13},{... | collective-permute-start | bytes 599048 | tf_op jit(solution)/shard_map/ppermute | solution.py:39
  97.6 23.3 %collective-permute-start.13 = (bf16[4,3,128,65]{2,3,1,0:T(8,128)(2,1)S(1)}, bf16[4,3,128,65]{2,3,1,0:T(8,128)(2,1)S(1)}, u32[]{:S(2)}, u32[]{:S(2)}) collective-permute-start(bf16[4,3,128,65]{2,3,1,0:T(8,128)(2,1)S(1)} %convolution_convert_fusion.1), channel_id=1, source_target_pairs={{0,2},{1,3},{4,6},{5,7},{8,10},{9,11},{12,14},{13,15},{16,18},{17,... | collective-permute-start | bytes 599048 | tf_op jit(solution)/shard_map/ppermute | solution.py:39
  99.5 19.6 %collective-permute-start.14 = (bf16[4,3,128,65]{2,3,1,0:T(8,128)(2,1)S(1)}, bf16[4,3,128,65]{2,3,1,0:T(8,128)(2,1)S(1)}, u32[]{:S(2)}, u32[]{:S(2)}) collective-permute-start(bf16[4,3,128,65]{2,3,1,0:T(8,128)(2,1)S(1)} %convolution_convert_fusion.1), channel_id=1, source_target_pairs={{0,3},{4,7},{8,11},{12,15},{16,19},{20,23},{24,27},{28,31}} | collective-permute-start | bytes 599048 | tf_op jit(solution)/shard_map/ppermute | solution.py:39
  164.1 33.4 %collective-permute-start.24 = (bf16[4,3,128,65]{2,3,1,0:T(8,128)(2,1)S(1)}, bf16[4,3,128,65]{2,3,1,0:T(8,128)(2,1)S(1)}, u32[]{:S(2)}, u32[]{:S(2)}) collective-permute-start(bf16[4,3,128,65]{2,3,1,0:T(8,128)(2,1)S(1)} %convolution_convert_fusion), channel_id=1, source_target_pairs={{1,0},{2,1},{3,2},{5,4},{6,5},{7,6},{9,8},{10,9},{11,10},{13,12},{... | collective-permute-start | bytes 599048 | tf_op jit(solution)/shard_map/ppermute | solution.py:39
  165.6 31.9 %collective-permute-start.25 = (bf16[4,3,128,65]{2,3,1,0:T(8,128)(2,1)S(1)}, bf16[4,3,128,65]{2,3,1,0:T(8,128)(2,1)S(1)}, u32[]{:S(2)}, u32[]{:S(2)}) collective-permute-start(bf16[4,3,128,65]{2,3,1,0:T(8,128)(2,1)S(1)} %convolution_convert_fusion), channel_id=1, source_target_pairs={{2,0},{3,1},{6,4},{7,5},{10,8},{11,9},{14,12},{15,13},{18,16},{19,... | collective-permute-start | bytes 599048 | tf_op jit(solution)/shard_map/ppermute | solution.py:39
  166.9 30.5 %collective-permute-start.26 = (bf16[4,3,128,65]{2,3,1,0:T(8,128)(2,1)S(1)}, bf16[4,3,128,65]{2,3,1,0:T(8,128)(2,1)S(1)}, u32[]{:S(2)}, u32[]{:S(2)}) collective-permute-start(bf16[4,3,128,65]{2,3,1,0:T(8,128)(2,1)S(1)} %convolution_convert_fusion), channel_id=1, source_target_pairs={{3,0},{7,4},{11,8},{15,12},{19,16},{23,20},{27,24},{31,28}} | collective-permute-start | bytes 599048 | tf_op jit(solution)/shard_map/ppermute | solution.py:39
  186.7 19.9 %collective-permute-start.36 = (bf16[4,2,2,24,768]{4,3,2,1,0:T(8,128)(2,1)S(1)}, bf16[4,2,2,24,768]{4,3,2,1,0:T(8,128)(2,1)S(1)}, u32[]{:S(2)}, u32[]{:S(2)}) collective-permute-start(bf16[4,2,2,24,768]{4,3,2,1,0:T(8,128)(2,1)S(1)} %fusion.68), channel_id=1, source_target_pairs={{0,4},{4,0},{8,12},{12,8},{16,20},{20,16},{24,28},{28,24},{1,5},{5... | collective-permute-start | bytes 1769480 | tf_op jit(solution)/shard_map/ppermute | solution.py:30
  191.1 65.5 %collective-permute-start.45 = (bf16[4,2,2,96,768]{4,3,0,2,1:T(8,128)(2,1)}, bf16[4,2,2,96,768]{4,3,0,2,1:T(8,128)(2,1)}, u32[]{:S(2)}, u32[]{:S(2)}) collective-permute-start(bf16[4,2,2,96,768]{4,3,0,2,1:T(8,128)(2,1)} %fusion.8), channel_id=1, source_target_pairs={{0,4},{4,0},{8,12},{12,8},{16,20},{20,16},{24,28},{28,24},{1,5},{5... | collective-permute-start | bytes 7077896 | tf_op jit(solution)/shard_map/ppermute | solution.py:30
  206.7 19.1 %collective-permute-start.37 = (bf16[4,2,24,768]{3,2,1,0:T(8,128)(2,1)S(1)}, bf16[4,2,24,768]{3,2,1,0:T(8,128)(2,1)S(1)}, u32[]{:S(2)}, u32[]{:S(2)}) collective-permute-start(bf16[4,2,24,768]{3,2,1,0:T(8,128)(2,1)S(1)} %fusion.74), channel_id=1, source_target_pairs={{0,8},{4,12},{8,0},{12,4},{16,24},{20,28},{24,16},{28,20},{1,9},{5... | collective-permute-start | bytes 884744 | tf_op jit(solution)/shard_map/ppermute | solution.py:30
  225.1 26.0 %collective-permute-start.27 = (bf16[4,2,2,96,576]{4,3,2,1,0:T(8,128)(2,1)}, bf16[4,2,2,96,576]{4,3,2,1,0:T(8,128)(2,1)}, u32[]{:S(2)}, u32[]{:S(2)}) collective-permute-start(bf16[4,2,2,96,576]{4,3,2,1,0:T(8,128)(2,1)} %fusion.13), channel_id=1, source_target_pairs={{0,4},{4,0},{8,12},{12,8},{16,20},{20,16},{24,28},{28,24},{1,5},{5... | collective-permute-start | bytes 5308424 | tf_op jit(solution)/shard_map/ppermute | solution.py:30
  233.3 7.0 %collective-permute-start.40 = (bf16[24,768]{1,0:T(8,128)(2,1)S(1)}, bf16[24,768]{1,0:T(8,128)(2,1)S(1)}, u32[]{:S(2)}, u32[]{:S(2)}) collective-permute-start(bf16[24,768]{1,0:T(8,128)(2,1)S(1)} %get-tuple-element.155), channel_id=1, source_target_pairs={{0,2},{1,3},{2,0},{3,1},{4,6},{5,7},{6,4},{7,5},{8,10},{9,11},{10,... | collective-permute-start | bytes 110600 | tf_op jit(solution)/shard_map/ppermute | solution.py:34
  238.3 43.5 %collective-permute-start.54 = (bf16[4,2,2,96,768]{4,3,0,2,1:T(8,128)(2,1)}, bf16[4,2,2,96,768]{4,3,0,2,1:T(8,128)(2,1)S(1)}, u32[]{:S(2)}, u32[]{:S(2)}) collective-permute-start(bf16[4,2,2,96,768]{4,3,0,2,1:T(8,128)(2,1)} %fusion.9), channel_id=1, source_target_pairs={{0,4},{4,0},{8,12},{12,8},{16,20},{20,16},{24,28},{28,24},{1,5},{5... | collective-permute-start | bytes 7077896 | tf_op jit(solution)/shard_map/ppermute | solution.py:30
  246.9 8.8 %collective-permute-start.44 = (bf16[2,2,24,768]{3,2,1,0:T(8,128)(2,1)S(1)}, bf16[2,2,24,768]{3,2,1,0:T(8,128)(2,1)S(1)}, u32[]{:S(2)}, u32[]{:S(2)}) collective-permute-start(bf16[2,2,24,768]{3,2,1,0:T(8,128)(2,1)S(1)} %maximum_select_fusion.33), channel_id=1, source_target_pairs={{0,4},{4,0},{8,12},{12,8},{16,20},{20,16},{24,28},{28,24},{1,5},{5... | collective-permute-start | bytes 442376 | tf_op jit(solution)/shard_map/ppermute | solution.py:30
  254.4 24.1 %collective-permute-start.28 = (bf16[4,2,96,576]{3,2,1,0:T(8,128)(2,1)S(1)}, bf16[4,2,96,576]{3,2,1,0:T(8,128)(2,1)S(1)}, u32[]{:S(2)}, u32[]{:S(2)}) collective-permute-start(bf16[4,2,96,576]{3,2,1,0:T(8,128)(2,1)S(1)} %fusion.43), channel_id=1, source_target_pairs={{0,16},{4,20},{8,24},{12,28},{16,0},{20,4},{24,8},{28,12},{1,17},{... | collective-permute-start | bytes 2654216 | tf_op jit(solution)/shard_map/ppermute | solution.py:30
  278.7 14.5 %collective-permute-start.29 = (bf16[4,96,576]{2,1,0:T(8,128)(2,1)S(1)}, bf16[4,96,576]{2,1,0:T(8,128)(2,1)S(1)}, u32[]{:S(2)}, u32[]{:S(2)}) collective-permute-start(bf16[4,96,576]{2,1,0:T(8,128)(2,1)S(1)} %fusion.72), channel_id=1, source_target_pairs={{0,8},{4,12},{8,0},{12,4},{16,24},{20,28},{24,16},{28,20},{1,9},{5... | collective-permute-start | bytes 1327112 | tf_op jit(solution)/shard_map/ppermute | solution.py:30
  280.5 46.0 %collective-permute-start.46 = (bf16[4,2,96,768]{3,2,0,1:T(8,128)(2,1)}, bf16[4,2,96,768]{3,2,0,1:T(8,128)(2,1)}, u32[]{:S(2)}, u32[]{:S(2)}) collective-permute-start(bf16[4,2,96,768]{3,2,0,1:T(8,128)(2,1)} %fusion.40), channel_id=1, source_target_pairs={{0,16},{4,20},{8,24},{12,28},{16,0},{20,4},{24,8},{28,12},{1,17},{... | collective-permute-start | bytes 3538952 | tf_op jit(solution)/shard_map/ppermute | solution.py:30
  293.4 7.7 %collective-permute-start.32 = (bf16[96,576]{1,0:T(8,128)(2,1)S(1)}, bf16[96,576]{1,0:T(8,128)(2,1)S(1)}, u32[]{:S(2)}, u32[]{:S(2)}) collective-permute-start(bf16[96,576]{1,0:T(8,128)(2,1)S(1)} %get-tuple-element.139), channel_id=1, source_target_pairs={{0,1},{1,2},{2,3},{3,0},{4,5},{5,6},{6,7},{7,4},{8,9},{9,10},{10,1... | collective-permute-start | bytes 331784 | tf_op jit(solution)/shard_map/ppermute | solution.py:34
  293.5 9.5 %collective-permute-start.31 = (bf16[96,576]{1,0:T(8,128)(2,1)S(1)}, bf16[96,576]{1,0:T(8,128)(2,1)S(1)}, u32[]{:S(2)}, u32[]{:S(2)}) collective-permute-start(bf16[96,576]{1,0:T(8,128)(2,1)S(1)} %get-tuple-element.140), channel_id=1, source_target_pairs={{0,2},{1,3},{2,0},{3,1},{4,6},{5,7},{6,4},{7,5},{8,10},{9,11},{10,... | collective-permute-start | bytes 331784 | tf_op jit(solution)/shard_map/ppermute | solution.py:34
  295.7 7.3 %collective-permute-start.30 = (bf16[96,576]{1,0:T(8,128)(2,1)S(1)}, bf16[96,576]{1,0:T(8,128)(2,1)S(1)}, u32[]{:S(2)}, u32[]{:S(2)}) collective-permute-start(bf16[96,576]{1,0:T(8,128)(2,1)S(1)} %get-tuple-element.138), channel_id=1, source_target_pairs={{0,3},{1,0},{2,1},{3,2},{4,7},{5,4},{6,5},{7,6},{8,11},{9,8},{10,9... | collective-permute-start | bytes 331784 | tf_op jit(solution)/shard_map/ppermute | solution.py:34
  296.9 32.9 %collective-permute-start.55 = (bf16[4,2,96,768]{3,2,0,1:T(8,128)(2,1)S(1)}, bf16[4,2,96,768]{3,2,0,1:T(8,128)(2,1)}, u32[]{:S(2)}, u32[]{:S(2)}) collective-permute-start(bf16[4,2,96,768]{3,2,0,1:T(8,128)(2,1)S(1)} %fusion.41), channel_id=1, source_target_pairs={{0,8},{4,12},{8,0},{12,4},{16,24},{20,28},{24,16},{28,20},{1,9},{5... | collective-permute-start | bytes 3538952 | tf_op jit(solution)/shard_map/ppermute | solution.py:30
  303.0 22.0 %collective-permute-start.33 = (bf16[96,576]{1,0:T(8,128)(2,1)S(1)}, bf16[96,576]{1,0:T(8,128)(2,1)S(1)}, u32[]{:S(2)}, u32[]{:S(2)}) collective-permute-start(bf16[96,576]{1,0:T(8,128)(2,1)S(1)} %fusion.86), channel_id=1, source_target_pairs={{0,8},{4,12},{8,0},{12,4},{16,24},{20,28},{24,16},{28,20},{1,9},{5... | collective-permute-start | bytes 331784 | tf_op jit(solution)/shard_map/ppermute | solution.py:30
  329.1 11.7 %collective-permute-start.47 = (bf16[4,96,768]{2,1,0:T(8,128)(2,1)S(1)}, bf16[4,96,768]{2,1,0:T(8,128)(2,1)S(1)}, u32[]{:S(2)}, u32[]{:S(2)}) collective-permute-start(bf16[4,96,768]{2,1,0:T(8,128)(2,1)S(1)} %fusion.69), channel_id=1, source_target_pairs={{0,8},{4,12},{8,0},{12,4},{16,24},{20,28},{24,16},{28,20},{1,9},{5... | collective-permute-start | bytes 1769480 | tf_op jit(solution)/shard_map/ppermute | solution.py:30
  331.6 12.8 %collective-permute-start.56 = (bf16[4,96,768]{2,1,0:T(8,128)(2,1)S(1)}, bf16[4,96,768]{2,1,0:T(8,128)(2,1)S(1)}, u32[]{:S(2)}, u32[]{:S(2)}) collective-permute-start(bf16[4,96,768]{2,1,0:T(8,128)(2,1)S(1)} %fusion.70), channel_id=1, source_target_pairs={{0,16},{4,20},{8,24},{12,28},{16,0},{20,4},{24,8},{28,12},{1,17},{... | collective-permute-start | bytes 1769480 | tf_op jit(solution)/shard_map/ppermute | solution.py:30
  332.1 12.8 %collective-permute-start.35 = (bf16[2,2,96,576]{3,2,1,0:T(8,128)(2,1)S(1)}, bf16[2,2,96,576]{3,2,1,0:T(8,128)(2,1)S(1)}, u32[]{:S(2)}, u32[]{:S(2)}) collective-permute-start(bf16[2,2,96,576]{3,2,1,0:T(8,128)(2,1)S(1)} %maximum_select_fusion.24), channel_id=1, source_target_pairs={{0,4},{4,0},{8,12},{12,8},{16,20},{20,16},{24,28},{28,24},{1,5},{5... | collective-permute-start | bytes 1327112 | tf_op jit(solution)/shard_map/ppermute | solution.py:30
  341.0 8.1 %collective-permute-start.49 = (bf16[96,768]{1,0:T(8,128)(2,1)S(1)}, bf16[96,768]{1,0:T(8,128)(2,1)S(1)}, u32[]{:S(2)}, u32[]{:S(2)}) collective-permute-start(bf16[96,768]{1,0:T(8,128)(2,1)S(1)} %get-tuple-element.137), channel_id=1, source_target_pairs={{0,2},{1,3},{2,0},{3,1},{4,6},{5,7},{6,4},{7,5},{8,10},{9,11},{10,... | collective-permute-start | bytes 442376 | tf_op jit(solution)/shard_map/ppermute | solution.py:34
  342.1 7.1 %collective-permute-start.48 = (bf16[96,768]{1,0:T(8,128)(2,1)S(1)}, bf16[96,768]{1,0:T(8,128)(2,1)S(1)}, u32[]{:S(2)}, u32[]{:S(2)}) collective-permute-start(bf16[96,768]{1,0:T(8,128)(2,1)S(1)} %get-tuple-element.135), channel_id=1, source_target_pairs={{0,3},{1,0},{2,1},{3,2},{4,7},{5,4},{6,5},{7,6},{8,11},{9,8},{10,9... | collective-permute-start | bytes 442376 | tf_op jit(solution)/shard_map/ppermute | solution.py:34
  344.6 8.8 %collective-permute-start.59 = (bf16[96,768]{1,0:T(8,128)(2,1)S(1)}, bf16[96,768]{1,0:T(8,128)(2,1)S(1)}, u32[]{:S(2)}, u32[]{:S(2)}) collective-permute-start(bf16[96,768]{1,0:T(8,128)(2,1)S(1)} %get-tuple-element.133), channel_id=1, source_target_pairs={{0,1},{1,2},{2,3},{3,0},{4,5},{5,6},{6,7},{7,4},{8,9},{9,10},{10,1... | collective-permute-start | bytes 442376 | tf_op jit(solution)/shard_map/ppermute | solution.py:34
  344.8 19.8 %collective-permute-start.58 = (bf16[96,768]{1,0:T(8,128)(2,1)S(1)}, bf16[96,768]{1,0:T(8,128)(2,1)S(1)}, u32[]{:S(2)}, u32[]{:S(2)}) collective-permute-start(bf16[96,768]{1,0:T(8,128)(2,1)S(1)} %get-tuple-element.134), channel_id=1, source_target_pairs={{0,2},{1,3},{2,0},{3,1},{4,6},{5,7},{6,4},{7,5},{8,10},{9,11},{10,... | collective-permute-start | bytes 442376 | tf_op jit(solution)/shard_map/ppermute | solution.py:34
  347.0 17.6 %collective-permute-start.57 = (bf16[96,768]{1,0:T(8,128)(2,1)S(1)}, bf16[96,768]{1,0:T(8,128)(2,1)S(1)}, u32[]{:S(2)}, u32[]{:S(2)}) collective-permute-start(bf16[96,768]{1,0:T(8,128)(2,1)S(1)} %get-tuple-element.132), channel_id=1, source_target_pairs={{0,3},{1,0},{2,1},{3,2},{4,7},{5,4},{6,5},{7,6},{8,11},{9,8},{10,9... | collective-permute-start | bytes 442376 | tf_op jit(solution)/shard_map/ppermute | solution.py:34
  349.2 18.0 %collective-permute-start.51 = (bf16[96,768]{1,0:T(8,128)(2,1)S(1)}, bf16[96,768]{1,0:T(8,128)(2,1)S(1)}, u32[]{:S(2)}, u32[]{:S(2)}) collective-permute-start(bf16[96,768]{1,0:T(8,128)(2,1)S(1)} %fusion.82), channel_id=1, source_target_pairs={{0,8},{4,12},{8,0},{12,4},{16,24},{20,28},{24,16},{28,20},{1,9},{5... | collective-permute-start | bytes 442376 | tf_op jit(solution)/shard_map/ppermute | solution.py:30
  368.8 9.9 %collective-permute-start.61 = (bf16[2,96,768]{2,1,0:T(8,128)(2,1)S(1)}, bf16[2,96,768]{2,1,0:T(8,128)(2,1)S(1)}, u32[]{:S(2)}, u32[]{:S(2)}) collective-permute-start(bf16[2,96,768]{2,1,0:T(8,128)(2,1)S(1)} %maximum_select_fusion.29), channel_id=1, source_target_pairs={{0,8},{4,12},{8,0},{12,4},{16,24},{20,28},{24,16},{28,20},{1,9},{5... | collective-permute-start | bytes 884744 | tf_op jit(solution)/shard_map/ppermute | solution.py:30
  374.4 8.0 %collective-permute-start.53 = (bf16[2,2,96,768]{3,2,1,0:T(8,128)(2,1)S(1)}, bf16[2,2,96,768]{3,2,1,0:T(8,128)(2,1)S(1)}, u32[]{:S(2)}, u32[]{:S(2)}) collective-permute-start(bf16[2,2,96,768]{3,2,1,0:T(8,128)(2,1)S(1)} %maximum_select_fusion.17), channel_id=1, source_target_pairs={{0,4},{4,0},{8,12},{12,8},{16,20},{20,16},{24,28},{28,24},{1,5},{5... | collective-permute-start | bytes 1769480 | tf_op jit(solution)/shard_map/ppermute | solution.py:30
  (43 other events, 401.1 us)
Sparse Core Ops, SparseCore 0:
  242.8 56.1 all-gather.3
